TPU v7x, 128 devices: a whole 4x4x4 slice. The times are simulated.
128 devices in a mesh: depth: 8 (over x, core), tile: 16 (over z, y).
Axes of the slice: x: 4, y: 4, z: 4, core: 2. Of those that a mesh axis runs over, the one named last changes fastest.
Arguments:
- velocity: float32 [3, 128, 512, 2048], P(None, 'depth', 'tile'), may hold values from -6 to 6
- view_sign: int32 [16], P('tile'), may hold values from 0 to 1, as said below
- brick_flags: int32 [16, 128, 16], P('depth', 'tile'), may hold values from 0 to 1, as said below
Outputs:
- image_color: float32 [3, 512, 2048], P(None, 'tile', 'depth')
- image_alpha: float32 [512, 2048], P('tile', 'depth')
Inputs may be any that keep to these rules, and one draw needn't show every extreme that they name: `view_sign`: 0 views a band of 32 image rows from the first index along the first dimension, 1 from its last; exactly half of the bands hold 1. `brick_flags`: 1 marks a brick that is rendered, 0 a brick that is treated as empty.
All inputs are finite; a program needn't handle non-finite values.
Results may differ from a plain program's by a relative error of at most 0.00005.
Values sent between devices are 32-bit elements; how exact they have to be, the bound alone decides.
A program may use at most 192 MiB of HBM per device.

v0:
```python
import jax
import jax.numpy as jnp
from jax import lax
from jax.sharding import PartitionSpec as P

ALPHA_PEAK = 0.04


def with_halo(cells, sides, width):
    for axis, dim in sides:
        count = lax.axis_size(axis)
        ends = count - 1
        head = lax.slice_in_dim(cells, 0, width, axis=dim)
        tail = lax.slice_in_dim(cells, cells.shape[dim] - width, cells.shape[dim], axis=dim)
        cells = jnp.concatenate(
            [
                lax.ppermute(tail, axis, [(i, (i + 1) % count) for i in range(ends)]),
                cells,
                lax.ppermute(head, axis, [((i + 1) % count, i) for i in range(ends)]),
            ],
            axis=dim,
        )
    return cells


def from_partner(value, axis, bit):
    mask = 2**bit
    pairs = [(source, source ^ mask) for source in range(lax.axis_size(axis))]
    return lax.ppermute(value, axis, pairs)


def stencil_valid(padded, along_dim):
    length = padded.shape[along_dim] - 4
    shifted = [lax.slice_in_dim(padded, k, k + length, axis=along_dim) for k in range(5)]
    return (shifted[0] - 8.0 * shifted[1] + 8.0 * shifted[3] - shifted[4]) / 12.0


def gradients(extended):
    gradient = []
    for i in range(3):
        component = extended[i]
        inner = component[2:-2, 2:-2]
        grad_x = stencil_valid(component[:, 2:-2], 0)
        grad_y = stencil_valid(component[2:-2], 1)
        grad_z = stencil_valid(jnp.pad(inner, ((0, 0), (0, 0), (2, 2))), 2)
        gradient.append([grad_x, grad_y, grad_z])
    return gradient


def qcriterion(gradient):
    diagonal = (
        gradient[0][0] * gradient[0][0]
        + gradient[1][1] * gradient[1][1]
        + gradient[2][2] * gradient[2][2]
    )
    crossed = (
        gradient[0][1] * gradient[1][0]
        + gradient[0][2] * gradient[2][0]
        + gradient[1][2] * gradient[2][1]
    )
    return -0.5 * (diagonal + 2.0 * crossed)


def blur_valid(padded, along_dim):
    length = padded.shape[along_dim] - 2
    return (
        0.25 * lax.slice_in_dim(padded, 0, length, axis=along_dim)
        + 0.5 * lax.slice_in_dim(padded, 1, length + 1, axis=along_dim)
        + 0.25 * lax.slice_in_dim(padded, 2, length + 2, axis=along_dim)
    )


def per_device(velocity, view_sign, brick_flags):
    cells_x = velocity.shape[1]
    cells_y = velocity.shape[2]
    cells_z = velocity.shape[3]
    extended = with_halo(velocity, (("depth", 1), ("tile", 2)), 2)
    qfield = qcriterion(gradients(extended))
    qwide = with_halo(qfield, (("depth", 0), ("tile", 1)), 1)
    smooth_x = blur_valid(qwide, 0)
    smooth_y = blur_valid(smooth_x, 1)
    qsmooth = blur_valid(jnp.pad(smooth_y, ((0, 0), (0, 0), (1, 1))), 2)
    speed_sq = jnp.sum(velocity * velocity, axis=0)
    base = ALPHA_PEAK * jax.nn.sigmoid(2.0 * qsmooth)
    flag_six = brick_flags.astype(jnp.float32)[:, None, :, None, :, None]
    opacity = (
        base.reshape(cells_x // 8, 8, cells_y // 4, 4, cells_z // 128, 128) * flag_six
    ).reshape(cells_x, cells_y, cells_z)
    colour = (
        jnp.stack(
            [
                jax.nn.sigmoid(qsmooth),
                jax.nn.sigmoid(speed_sq - 3.0),
                jax.nn.sigmoid(-2.0 * qsmooth),
            ]
        )
        * opacity[None]
    )
    flipped = view_sign[0] == 1
    opacity = jnp.where(flipped, opacity[::-1], opacity)
    colour = jnp.where(flipped, colour[:, ::-1], colour)
    transmit = jnp.cumprod(1.0 - opacity, axis=0)
    before = jnp.concatenate([jnp.ones_like(transmit[:1]), transmit[:-1]], axis=0)
    local_color = jnp.sum(before[None] * colour, axis=1)
    local_trans = transmit[-1]
    depth_count = lax.axis_size("depth")
    piece_width = cells_z // depth_count
    current_c = local_color.reshape(3, cells_y, depth_count, piece_width)
    current_t = local_trans.reshape(1, cells_y, depth_count, piece_width)
    position = lax.axis_index("depth")
    for level_bit in range(depth_count.bit_length() - 1):
        half_count = current_c.shape[2] // 2
        view_c = current_c.reshape(3, cells_y, half_count, 2, piece_width)
        view_t = current_t.reshape(1, cells_y, half_count, 2, piece_width)
        is_lower = position >> level_bit & 1 == 0
        keep_c = jnp.where(is_lower, view_c[:, :, :, 0], view_c[:, :, :, 1])
        keep_t = jnp.where(is_lower, view_t[:, :, :, 0], view_t[:, :, :, 1])
        give_c = jnp.where(is_lower, view_c[:, :, :, 1], view_c[:, :, :, 0])
        give_t = jnp.where(is_lower, view_t[:, :, :, 1], view_t[:, :, :, 0])
        recv_c, recv_t = from_partner((give_c, give_t), "depth", level_bit)
        mine_front = is_lower != flipped
        front_c = jnp.where(mine_front, keep_c, recv_c)
        front_t = jnp.where(mine_front, keep_t, recv_t)
        back_c = jnp.where(mine_front, recv_c, keep_c)
        back_t = jnp.where(mine_front, recv_t, keep_t)
        current_c = front_c + front_t * back_c
        current_t = front_t * back_t
    image_color = current_c.reshape(3, cells_y, piece_width)
    final_trans = current_t.reshape(cells_y, piece_width)
    return (image_color, 1.0 - final_trans)


def solution(mesh):
    placed = (P(None, "depth", "tile", None), P("tile"), P("depth", "tile", None))
    return jax.shard_map(
        per_device,
        mesh=mesh,
        in_specs=placed,
        out_specs=(P(None, "tile", "depth"), P("tile", "depth")),
        check_vma=False,
    )
```

profile of v0, /device:TPU:96, one launch (start us, length us, event | category | flops | bytes accessed | tf_op | source)
XLA Modules:
  0.0 303.7 jit_solution(12951745004351988462)
XLA Ops:
  0.6 2.1 fusion.54
  8.8 14.4 %multiply_reduce_fusion = (f32[16,32,2048]{2,1,0:T(8,128)}, f32[3,20,32,2048]{3,2,1,0:T(8,128)}) fusion(f32[3,16,32,2048]{3,2,1,0:T(8,128)} %param.3, f32[3,20,32,2048]{3,2,1,0:T(8,128)} %constant_dynamic-update-slice_fusion.2), kind=kLoop, calls=%fused_computation.5 | loop fusion | flops 5242880 | bytes 29360128 | tf_op jit(solution)/shard_map/reduce_sum | solution.py:83
  24.6 4.3 %fusion.53 = (f32[3,20,2,2048]{3,2,1,0:T(2,128)S(1)}, f32[3,20,2,2048]{3,2,1,0:T(2,128)S(1)}) fusion(f32[3,20,32,2048]{3,2,1,0:T(8,128)} %constant_dynamic-update-slice_fusion), kind=kLoop, calls=%fused_computation.125 | loop fusion | bytes 3932160 | tf_op jit(solution)/shard_map/slice | solution.py:14
  29.5 4.8 %collective-permute-start.3 = (f32[3,20,2,2048]{3,1,2,0:T(8,128)S(1)}, f32[3,20,2,2048]{3,1,2,0:T(8,128)S(1)}, u32[]{:S(2)}, u32[]{:S(2)}) collective-permute-start(f32[3,20,2,2048]{3,1,2,0:T(8,128)S(1)} %copy.56), channel_id=1, source_target_pairs={{1,0},{2,1},{3,2},{4,3},{5,4},{6,5},{7,6},{8,7},{9,8},{10,9},{11,1... | collective-permute-start | bytes 2949128 | tf_op jit(solution)/shard_map/ppermute | solution.py:19
  37.0 11.0 %collective-permute-done.3 = f32[3,20,2,2048]{3,1,2,0:T(8,128)S(1)} collective-permute-done((f32[3,20,2,2048]{3,1,2,0:T(8,128)S(1)}, f32[3,20,2,2048]{3,1,2,0:T(8,128)S(1)}, u32[]{:S(2)}, u32[]{:S(2)}) %collective-permute-start.3) | collective-permute-done | bytes 983072 | tf_op jit(solution)/shard_map/ppermute | solution.py:19
  48.7 6.3 %collective-permute-done.2 = f32[3,20,2,2048]{3,1,2,0:T(8,128)S(1)} collective-permute-done((f32[3,20,2,2048]{3,1,2,0:T(8,128)S(1)}, f32[3,20,2,2048]{3,1,2,0:T(8,128)S(1)}, u32[]{:S(2)}, u32[]{:S(2)}) %collective-permute-start.2) | collective-permute-done | bytes 983072 | tf_op jit(solution)/shard_map/ppermute | solution.py:17
  55.8 14.8 %pad_maximum_fusion = f32[3,20,36,2048]{3,2,1,0:T(8,128)} fusion(f32[3,20,2,2048]{3,2,1,0:T(2,128)S(1)} %copy.58, f32[3,20,32,2048]{3,2,1,0:T(8,128)} %constant_dynamic-update-slice_fusion, f32[3,20,2,2048]{3,2,1,0:T(2,128)S(1)} %copy.57), kind=kLoop, calls=%fused_computation | loop fusion | flops 8847360 | bytes 35389440 | tf_op jit(solution)/shard_map/concatenate | solution.py:15
  70.6 11.8 %slice_bitcast_fusion.5 = (f32[16,36,2048]{2,1,0:T(8,128)}, f32[16,36,2048]{2,1,0:T(8,128)}, f32[16,36,2048]{2,1,0:T(8,128)}) fusion(f32[3,20,36,2048]{3,2,1,0:T(8,128)} %pad_maximum_fusion), kind=kLoop, calls=%fused_computation.18 | loop fusion | bytes 28311552 | tf_op jit(solution)/shard_map/slice | solution.py:44
  82.4 11.9 %slice_bitcast_fusion.2 = (f32[20,36,2048]{2,1,0:T(8,128)S(1)}, f32[20,36,2048]{2,1,0:T(8,128)}, f32[20,36,2048]{2,1,0:T(8,128)}) fusion(f32[3,20,36,2048]{3,2,1,0:T(8,128)} %pad_maximum_fusion), kind=kLoop, calls=%fused_computation.8 | loop fusion | bytes 35389440 | tf_op jit(solution)/shard_map/squeeze | solution.py:41
  94.3 5.4 %slice.372 = f32[16,32,2048]{2,1,0:T(8,128)} slice(f32[20,36,2048]{2,1,0:T(8,128)} %get-tuple-element.5), slice={[2:18], [2:34], [0:2048]} | slice | bytes 8388608 | tf_op jit(solution)/shard_map/slice | solution.py:42
  99.7 2.5 slice.367
  102.2 2.8 slice.356
  105.1 65.6 %fusion.16 = f32[16,32,2048]{2,1,0:T(8,128)S(1)} fusion(f32[16,36,2048]{2,1,0:T(8,128)} %get-tuple-element.8, f32[20,36,2048]{2,1,0:T(8,128)} %get-tuple-element.6, f32[20,36,2048]{2,1,0:T(8,128)} %get-tuple-element.5, f32[16,36,2048]{2,1,0:T(8,128)} %get-tuple-element.9, f32[16,36,2048]{2,1,0:T(8,128)} %get-tuple-element.7, ...), kind=kLoop, calls=%fused_computation.37 | loop fusion | flops 70254592 | bytes 117440512 | tf_op jit(solution)/shard_map/mul | solution.py:61
  172.0 17.2 %collective-permute-start.4 = (f32[1,32,2048]{2,1,0:T(8,128)S(1)}, f32[1,32,2048]{2,1,0:T(8,128)S(1)}, u32[]{:S(2)}, u32[]{:S(2)}) collective-permute-start(f32[1,32,2048]{2,1,0:T(8,128)S(1)} %get-tuple-element.20), channel_id=1, source_target_pairs={{0,16},{16,32},{32,48},{48,64},{64,80},{80,96},{96,112},{1,17},{17... | collective-permute-start | bytes 786440 | tf_op jit(solution)/shard_map/ppermute | solution.py:17
  193.2 4.1 %collective-permute-start.6 = (f32[18,1,2048]{2,1,0:T(1,128)S(1)}, f32[18,1,2048]{2,1,0:T(1,128)S(1)}, u32[]{:S(2)}, u32[]{:S(2)}) collective-permute-start(f32[18,1,2048]{2,1,0:T(1,128)S(1)} %get-tuple-element.16), channel_id=1, source_target_pairs={{0,1},{1,2},{2,3},{3,4},{4,5},{5,6},{6,7},{7,8},{8,9},{9,10},{10,1... | collective-permute-start | bytes 442376 | tf_op jit(solution)/shard_map/ppermute | solution.py:17
  197.3 2.4 mul.239
  199.8 5.0 %mul.240 = f32[16,32,2048]{2,1,0:T(8,128)} reshape(f32[2,8,8,4,16,128]{5,4,3,2,1,0:T(8,128)} %mul.239) | data formatting | bytes 8388608 | tf_op jit(solution)/shard_map/mul | solution.py:87
  205.4 2.8 pad_maximum_fusion.1
  210.0 3.2 %fusion.9 = f32[16,32,2048]{2,1,0:T(8,128)} fusion(f32[16,34,2048]{2,1,0:T(8,128)S(1)} %fusion.2), kind=kLoop, calls=%fused_computation.27 | loop fusion | flops 5242880 | bytes 16777216 | tf_op jit(solution)/shard_map/add | solution.py:67
  213.1 7.2 %multiply_multiply_fusion = (f32[16,32,2048]{2,1,0:T(8,128)S(1)}, f32[16,32,2048]{2,1,0:T(8,128)S(1)}) fusion(f32[16,32,2048]{2,1,0:T(8,128)S(1)} %copy-done.3, f32[16,32,2048]{2,1,0:T(8,128)} %fusion.9), kind=kLoop, calls=%fused_computation.82 | loop fusion | flops 11534336 | bytes 16777216 | tf_op jit(solution)/shard_map/mul | solution.py:87
  221.2 14.2 %fusion.58 = f32[16,32,2048]{2,1,0:T(8,128)S(1)} fusion(f32[16,32,2048]{2,1,0:T(8,128)S(1)} %fusion.8), kind=kOutput, calls=%fused_computation.130 | output fusion | flops 15728640 | bytes 8388608 | tf_op jit(solution)/shard_map/jit(cumprod)/reduce_window | solution.py:102
  235.4 2.3 slice.386
  240.4 3.3 %divide_bitcast_fusion.2 = (f32[1,16,32,2048]{3,2,1,0:T(8,128)S(1)}, f32[1,16,32,2048]{3,2,1,0:T(8,128)S(1)}, f32[1,16,32,2048]{3,2,1,0:T(8,128)S(1)}) fusion(f32[16,32,2048]{2,1,0:T(8,128)S(1)} %get-tuple-element.3, f32[16,32,2048]{2,1,0:T(8,128)S(1)} %copy-done.1), kind=kLoop, calls=%fused_computation.81 | loop fusion | flops 11534336 | bytes 20971520 | tf_op jit(solution)/shard_map/stack | solution.py:90
  243.6 2.8 concatenate.19
  246.5 5.4 %maximum_multiply_fusion = f32[3,16,32,2048]{3,2,1,0:T(8,128)} fusion(f32[1,16,32,2048]{3,2,1,0:T(8,128)S(1)} %get-tuple-element.19, f32[1,16,32,2048]{3,2,1,0:T(8,128)S(1)} %get-tuple-element.33, f32[1,16,32,2048]{3,2,1,0:T(8,128)S(1)} %get-tuple-element.18, f32[16,32,2048]{2,1,0:T(8,128)S(1)} %get-tuple-element.2), kind=kLoop, calls=%fused_computation.4 | loop fusion | flops 9437184 | bytes 29360128 | tf_op jit(solution)/shard_map/mul | solution.py:90
  251.8 12.6 %fusion.1 = f32[3,32,2048]{2,1,0:T(8,128)} fusion(f32[3,16,32,2048]{3,2,1,0:T(8,128)} %maximum_multiply_fusion, f32[16,32,2048]{2,1,0:T(8,128)S(1)} %concatenate.19, pred[]{:T(512)} %bitcast), kind=kLoop, calls=%fused_computation.3 | loop fusion | flops 9240576 | bytes 17563648 | tf_op jit(solution)/shard_map/reduce_sum | solution.py:104
  266.7 16.1 %collective-permute-start.9 = (f32[1,32,4,256]{3,1,2,0:T(8,128)S(1)}, f32[1,32,4,256]{3,1,2,0:T(8,128)S(1)}, u32[]{:S(2)}, u32[]{:S(2)}) collective-permute-start(f32[1,32,4,256]{3,1,2,0:T(8,128)S(1)} %select_bitcast_fusion.1), channel_id=1, source_target_pairs={{0,16},{16,0},{32,48},{48,32},{64,80},{80,64},{96,112},{112,96},{1... | collective-permute-start | bytes 393224 | tf_op jit(solution)/shard_map/ppermute | solution.py:29
  283.8 3.4 %collective-permute-start.11 = (f32[1,32,2,256]{3,1,2,0:T(8,128)S(1)}, f32[1,32,2,256]{3,1,2,0:T(8,128)S(1)}, u32[]{:S(2)}, u32[]{:S(2)}) collective-permute-start(f32[1,32,2,256]{3,1,2,0:T(8,128)S(1)} %select_bitcast_fusion.3), channel_id=1, source_target_pairs={{0,32},{16,48},{32,0},{48,16},{64,96},{80,112},{96,64},{112,80},{1... | collective-permute-start | bytes 196616 | tf_op jit(solution)/shard_map/ppermute | solution.py:29
  287.4 2.3 collective-permute-done.11
  293.6 3.2 %collective-permute-done.10 = f32[3,32,2,256]{3,1,2,0:T(8,128)S(1)} collective-permute-done((f32[3,32,2,256]{3,1,2,0:T(8,128)S(1)}, f32[3,32,2,256]{3,1,2,0:T(8,128)S(1)}, u32[]{:S(2)}, u32[]{:S(2)}) %collective-permute-start.10) | collective-permute-done | bytes 196640 | tf_op jit(solution)/shard_map/ppermute | solution.py:29
  296.9 2.6 collective-permute-start.12
  300.1 3.0 collective-permute-done.12
  (63 shorter events, 31.3 us)
Async XLA Ops:
  2.7 4.8 %collective-permute-start = (f32[3,2,32,2048]{3,2,1,0:T(8,128)S(1)}, f32[3,2,32,2048]{3,2,1,0:T(8,128)S(1)}, u32[]{:S(2)}, u32[]{:S(2)}) collective-permute-start(f32[3,2,32,2048]{3,2,1,0:T(8,128)S(1)} %get-tuple-element.15), channel_id=1, source_target_pairs={{0,16},{16,32},{32,48},{48,64},{64,80},{80,96},{96,112},{1,17},{17... | collective-permute-start | bytes 4718600 | tf_op jit(solution)/shard_map/ppermute | solution.py:17
  4.6 18.7 %collective-permute-start.1 = (f32[3,2,32,2048]{3,2,1,0:T(8,128)S(1)}, f32[3,2,32,2048]{3,2,1,0:T(8,128)S(1)}, u32[]{:S(2)}, u32[]{:S(2)}) collective-permute-start(f32[3,2,32,2048]{3,2,1,0:T(8,128)S(1)} %get-tuple-element.14), channel_id=1, source_target_pairs={{16,0},{32,16},{48,32},{64,48},{80,64},{96,80},{112,96},{17,1},{33... | collective-permute-start | bytes 4718600 | tf_op jit(solution)/shard_map/ppermute | solution.py:19
  29.5 18.5 %collective-permute-start.3 = (f32[3,20,2,2048]{3,1,2,0:T(8,128)S(1)}, f32[3,20,2,2048]{3,1,2,0:T(8,128)S(1)}, u32[]{:S(2)}, u32[]{:S(2)}) collective-permute-start(f32[3,20,2,2048]{3,1,2,0:T(8,128)S(1)} %copy.56), channel_id=1, source_target_pairs={{1,0},{2,1},{3,2},{4,3},{5,4},{6,5},{7,6},{8,7},{9,8},{10,9},{11,1... | collective-permute-start | bytes 2949128 | tf_op jit(solution)/shard_map/ppermute | solution.py:19
  34.8 20.2 %collective-permute-start.2 = (f32[3,20,2,2048]{3,1,2,0:T(8,128)S(1)}, f32[3,20,2,2048]{3,1,2,0:T(8,128)S(1)}, u32[]{:S(2)}, u32[]{:S(2)}) collective-permute-start(f32[3,20,2,2048]{3,1,2,0:T(8,128)S(1)} %copy.55), channel_id=1, source_target_pairs={{0,1},{1,2},{2,3},{3,4},{4,5},{5,6},{6,7},{7,8},{8,9},{9,10},{10,1... | collective-permute-start | bytes 2949128 | tf_op jit(solution)/shard_map/ppermute | solution.py:17
  94.3 7.9 %slice-start = ((s8[6553600]{0:T(1024)(128)(4,1)}), s8[4194304]{0:T(1024)(128)(4,1)S(1)}, s32[]{:S(2)}) async-start(s8[6553600]{0:T(1024)(128)(4,1)} %bitcast.137), calls=%async_computation | async-start | bytes 8388608
  99.7 2.5 slice-start.1
  170.6 19.7 %copy-start = (f32[16,32,2048]{2,1,0:T(8,128)}, f32[16,32,2048]{2,1,0:T(8,128)S(1)}, u32[]{:S(2)}) copy-start(f32[16,32,2048]{2,1,0:T(8,128)S(1)} %fusion.16) | copy-start | bytes 12582916
  170.7 26.7 %copy-start.4 = (s32[2,8,16]{2,1,0:T(8,128)S(1)}, s32[2,8,16]{2,1,0:T(8,128)}, u32[]{:S(2)}) copy-start(s32[2,8,16]{2,1,0:T(8,128)} %param.5) | copy-start | bytes 3076
  170.7 18.5 %collective-permute-start.5 = (f32[1,32,2048]{2,1,0:T(8,128)S(1)}, f32[1,32,2048]{2,1,0:T(8,128)S(1)}, u32[]{:S(2)}, u32[]{:S(2)}) collective-permute-start(f32[1,32,2048]{2,1,0:T(8,128)S(1)} %get-tuple-element.21), channel_id=1, source_target_pairs={{16,0},{32,16},{48,32},{64,48},{80,64},{96,80},{112,96},{17,1},{33... | collective-permute-start | bytes 786440 | tf_op jit(solution)/shard_map/ppermute | solution.py:19
  172.0 18.4 %collective-permute-start.4 = (f32[1,32,2048]{2,1,0:T(8,128)S(1)}, f32[1,32,2048]{2,1,0:T(8,128)S(1)}, u32[]{:S(2)}, u32[]{:S(2)}) collective-permute-start(f32[1,32,2048]{2,1,0:T(8,128)S(1)} %get-tuple-element.20), channel_id=1, source_target_pairs={{0,16},{16,32},{32,48},{48,64},{64,80},{80,96},{96,112},{1,17},{17... | collective-permute-start | bytes 786440 | tf_op jit(solution)/shard_map/ppermute | solution.py:17
  191.2 14.2 %collective-permute-start.7 = (f32[18,1,2048]{2,1,0:T(1,128)}, f32[18,1,2048]{2,1,0:T(1,128)S(1)}, u32[]{:S(2)}, u32[]{:S(2)}) collective-permute-start(f32[18,1,2048]{2,1,0:T(1,128)} %get-tuple-element.17), channel_id=1, source_target_pairs={{1,0},{2,1},{3,2},{4,3},{5,4},{6,5},{7,6},{8,7},{9,8},{10,9},{11,1... | collective-permute-start | bytes 442376 | tf_op jit(solution)/shard_map/ppermute | solution.py:19
  193.2 12.3 %collective-permute-start.6 = (f32[18,1,2048]{2,1,0:T(1,128)S(1)}, f32[18,1,2048]{2,1,0:T(1,128)S(1)}, u32[]{:S(2)}, u32[]{:S(2)}) collective-permute-start(f32[18,1,2048]{2,1,0:T(1,128)S(1)} %get-tuple-element.16), channel_id=1, source_target_pairs={{0,1},{1,2},{2,3},{3,4},{4,5},{5,6},{6,7},{7,8},{8,9},{9,10},{10,1... | collective-permute-start | bytes 442376 | tf_op jit(solution)/shard_map/ppermute | solution.py:17
  209.9 3.2 %copy-start.3 = (f32[16,32,2048]{2,1,0:T(8,128)S(1)}, f32[16,32,2048]{2,1,0:T(8,128)}, u32[]{:S(2)}) copy-start(f32[16,32,2048]{2,1,0:T(8,128)} %mul.240) | copy-start | bytes 12582916
  235.3 4.0 %copy-start.2 = (f32[16,32,2048]{2,1,0:T(8,128)}, f32[16,32,2048]{2,1,0:T(8,128)S(1)}, u32[]{:S(2)}) copy-start(f32[16,32,2048]{2,1,0:T(8,128)S(1)} %fusion.58) | copy-start | bytes 12582916
  235.3 5.0 %copy-start.1 = (f32[16,32,2048]{2,1,0:T(8,128)S(1)}, f32[16,32,2048]{2,1,0:T(8,128)}, u32[]{:S(2)}) copy-start(f32[16,32,2048]{2,1,0:T(8,128)} %get-tuple-element.12) | copy-start | bytes 12582916
  251.8 14.4 %slice-start.2 = ((f32[16,32,2048]{2,1,0:T(8,128)}), f32[1,32,2048]{2,1,0:T(8,128)S(1)}, s32[]{:S(2)}) async-start(f32[16,32,2048]{2,1,0:T(8,128)} %copy-done.2), calls=%async_computation.2 | async-start | bytes 524288 | tf_op jit(solution)/shard_map/slice | solution.py:105
  266.7 17.1 %collective-permute-start.9 = (f32[1,32,4,256]{3,1,2,0:T(8,128)S(1)}, f32[1,32,4,256]{3,1,2,0:T(8,128)S(1)}, u32[]{:S(2)}, u32[]{:S(2)}) collective-permute-start(f32[1,32,4,256]{3,1,2,0:T(8,128)S(1)} %select_bitcast_fusion.1), channel_id=1, source_target_pairs={{0,16},{16,0},{32,48},{48,32},{64,80},{80,64},{96,112},{112,96},{1... | collective-permute-start | bytes 393224 | tf_op jit(solution)/shard_map/ppermute | solution.py:29
  283.6 6.0 %collective-permute-start.8 = (f32[3,32,4,256]{3,2,1,0:T(4,128)S(1)}, f32[3,32,4,256]{3,2,1,0:T(4,128)S(1)}, u32[]{:S(2)}, u32[]{:S(2)}) collective-permute-start(f32[3,32,4,256]{3,2,1,0:T(4,128)S(1)} %bitcast.143), channel_id=1, source_target_pairs={{0,16},{16,0},{32,48},{48,32},{64,80},{80,64},{96,112},{112,96},{1... | collective-permute-start | bytes 1179656 | tf_op jit(solution)/shard_map/ppermute | solution.py:29
  283.8 5.8 %collective-permute-start.11 = (f32[1,32,2,256]{3,1,2,0:T(8,128)S(1)}, f32[1,32,2,256]{3,1,2,0:T(8,128)S(1)}, u32[]{:S(2)}, u32[]{:S(2)}) collective-permute-start(f32[1,32,2,256]{3,1,2,0:T(8,128)S(1)} %select_bitcast_fusion.3), channel_id=1, source_target_pairs={{0,32},{16,48},{32,0},{48,16},{64,96},{80,112},{96,64},{112,80},{1... | collective-permute-start | bytes 196616 | tf_op jit(solution)/shard_map/ppermute | solution.py:29
  290.0 6.8 %collective-permute-start.10 = (f32[3,32,2,256]{3,1,2,0:T(8,128)S(1)}, f32[3,32,2,256]{3,1,2,0:T(8,128)S(1)}, u32[]{:S(2)}, u32[]{:S(2)}) collective-permute-start(f32[3,32,2,256]{3,1,2,0:T(8,128)S(1)} %select_bitcast_fusion), channel_id=1, source_target_pairs={{0,32},{16,48},{32,0},{48,16},{64,96},{80,112},{96,64},{112,80},{1... | collective-permute-start | bytes 589832 | tf_op jit(solution)/shard_map/ppermute | solution.py:29
  292.0 7.5 %collective-permute-start.13 = (f32[1,32,1,256]{3,1,2,0:T(8,128)S(1)}, f32[1,32,1,256]{3,1,2,0:T(8,128)S(1)}, u32[]{:S(2)}, u32[]{:S(2)}) collective-permute-start(f32[1,32,1,256]{3,1,2,0:T(8,128)S(1)} %select_bitcast_fusion.4), channel_id=1, source_target_pairs={{0,64},{16,80},{32,96},{48,112},{64,0},{80,16},{96,32},{112,48},{1... | collective-permute-start | bytes 98312 | tf_op jit(solution)/shard_map/ppermute | solution.py:29
  296.9 6.2 %collective-permute-start.12 = (f32[3,32,1,256]{3,1,0,2:T(8,128)S(1)}, f32[3,32,1,256]{3,1,0,2:T(8,128)S(1)}, u32[]{:S(2)}, u32[]{:S(2)}) collective-permute-start(f32[3,32,1,256]{3,1,0,2:T(8,128)S(1)} %select_bitcast_fusion.2), channel_id=1, source_target_pairs={{0,64},{16,80},{32,96},{48,112},{64,0},{80,16},{96,32},{112,48},{1... | collective-permute-start | bytes 294920 | tf_op jit(solution)/shard_map/ppermute | solution.py:29
where the time goes:
time: 304 us
  other arithmetic  149 us (49%)
  local copies, waits for them, and re-layouts  64 us (21%)
  starting transfers between devices  60.4 us (20%)
  waiting for transfers between devices  28.5 us (9%)
    mul x1, other arithmetic, qcriterion(): return -0.5 * (diagonal + 2.0 * crossed)  65.6 us
    ppermute x6, starting transfers between devices, from_partner(): return lax.ppermute(value, axis, pairs)  25.9 us
    ppermute x4, starting transfers between devices, with_halo(): lax.ppermute(tail, axis, [(i, (i + 1) % count) for i in range(ends)])  25.3 us
    concatenate x2, other arithmetic, with_halo(): jnp.concatenate([lax.ppermute(tail, axis, [(i, (i + 1) % count) for i in...  17.6 us
    reduce_sum x1, other arithmetic, per_device(): speed_sq = jnp.sum(velocity * velocity, axis=0)  14.4 us
    another operation x1, other arithmetic, per_device(): transmit = jnp.cumprod(1.0 - opacity, axis=0)  14.2 us
    reduce_sum x1, other arithmetic, per_device(): local_color = jnp.sum(before[None] * colour, axis=1)  12.6 us
    squeeze x1, local copies, waits for them, and re-layouts, gradients(): component = extended[i]  11.9 us
  transfers between devices with their start and end apart: 14, of which 8 were waited for; matrix products, arithmetic and copies ran while one was open for 9% of the time, Pallas kernels for 0%

commit v1 on v0

v1 whole, which is shorter than its diff:
```python
import jax
import jax.numpy as jnp
from jax import lax
from jax.experimental import pallas as pl
from jax.experimental.pallas import tpu as pltpu
from jax.sharding import PartitionSpec as P

ALPHA_PEAK = 0.04
MESH = pl.DeviceIdType.MESH
LANES = 128
HALF = 8
CHUNKS = 2 * HALF


def z_gradient(row):
    even, odd = row[:, :HALF], row[:, HALF:]
    lane = lax.broadcasted_iota(jnp.int32, even.shape, 2)
    sub = lax.broadcasted_iota(jnp.int32, even.shape, 1)
    after_odd = jnp.where(sub == HALF - 1, 0.0, pltpu.roll(even, HALF - 1, 1))
    before_even = jnp.where(sub == 0, 0.0, pltpu.roll(odd, 1, 1))
    halves = []
    for mine, after, before in ((even, odd, before_even), (odd, after_odd, even)):
        near = (pltpu.roll(jnp.where(lane < 1, after, mine), LANES - 1, 2)
                - pltpu.roll(jnp.where(lane >= LANES - 1, before, mine), 1, 2))
        far = (pltpu.roll(jnp.where(lane < 2, after, mine), LANES - 2, 2)
               - pltpu.roll(jnp.where(lane >= LANES - 2, before, mine), 2, 2))
        halves.append(8.0 * near - far)
    return jnp.concatenate(halves, axis=1)


def z_blur(row):
    even, odd = row[:, :HALF], row[:, HALF:]
    lane = lax.broadcasted_iota(jnp.int32, even.shape, 2)
    sub = lax.broadcasted_iota(jnp.int32, even.shape, 1)
    after_odd = jnp.where(sub == HALF - 1, 0.0, pltpu.roll(even, HALF - 1, 1))
    before_even = jnp.where(sub == 0, 0.0, pltpu.roll(odd, 1, 1))
    halves = []
    for mine, after, before in ((even, odd, before_even), (odd, after_odd, even)):
        ahead = jnp.where(lane < 1, after, mine)
        behind = jnp.where(lane >= LANES - 1, before, mine)
        halves.append(
            (pltpu.roll(ahead, LANES - 1, 2) + pltpu.roll(behind, 1, 2)) + 2.0 * mine
        )
    return jnp.concatenate(halves, axis=1)


def q_rows(u, q, x, y, rows):
    def parts(comp):
        span = u[comp, x + 2, pl.ds(y, rows + 4)]
        near_x = u[comp, x + 3, pl.ds(y + 2, rows)] - u[comp, x + 1, pl.ds(y + 2, rows)]
        far_x = u[comp, x + 4, pl.ds(y + 2, rows)] - u[comp, x, pl.ds(y + 2, rows)]
        near_y = span[3 : rows + 3] - span[1 : rows + 1]
        far_y = span[4:] - span[:rows]
        return (
            8.0 * near_x - far_x,
            8.0 * near_y - far_y,
            z_gradient(span[2 : rows + 2]),
        )

    g00, g01, g02 = parts(0)
    total = g00 * g00
    g10, g11, g12 = parts(1)
    total = total + g11 * g11
    cross = g01 * g10
    g20, g21, g22 = parts(2)
    total = total + g22 * g22
    cross = cross + g02 * g20 + g12 * g21
    q[x + 1, pl.ds(y + 1, rows)] = total + (cross + cross)


def kernel(
    nd, nt, cx, cy, vel, sign, bricks, color, alpha,
    u, q, flags, image, pieces, load_sem,
    xs_sem, xr_sem, ys_sem, yr_sem, qs_sem, qr_sem, is_sem, ir_sem, own_sem,
):
    depth, tile = lax.axis_index("depth"), lax.axis_index("tile")
    d_next, d_prev = lax.rem(depth + 1, nd), lax.rem(depth + nd - 1, nd)
    t_next, t_prev = lax.rem(tile + 1, nt), lax.rem(tile + nt - 1, nt)
    inner = cx - 4
    mid = cy - 4

    def load(group, x0, nx, y0, ny):
        for comp in range(3):
            for chunk in range(CHUNKS):
                pltpu.make_async_copy(
                    vel.at[comp, pl.ds(x0, nx), pl.ds(y0, ny), pl.ds(chunk * LANES, LANES)],
                    u.at[comp, pl.ds(x0 + 2, nx), pl.ds(y0 + 2, ny),
                         HALF * (chunk % 2) + chunk // 2],
                    load_sem.at[group],
                ).start()

    def loaded(group, x0, nx, y0, ny):
        where = u.at[:, pl.ds(x0 + 2, nx), pl.ds(y0 + 2, ny)]
        pltpu.make_async_copy(where, where, load_sem.at[group]).wait()

    faces = ((0, cx - 2, 2, 0, cy), (1, 0, 2, 0, cy))
    edges = ((2, 2, inner, 0, 8), (3, 2, inner, cy - 8, 8))
    middle = (4, 2, inner, 8, cy - 16)
    for group in faces + edges + (middle,):
        load(*group)

    around = [(d_next, tile), (d_prev, tile), (depth, t_next), (depth, t_prev),
              (d_next, t_next), (d_next, t_prev), (d_prev, t_next), (d_prev, t_prev)]
    around += [(lax.rem(depth + hop, nd), tile) for hop in range(2, nd - 1)]
    barrier = pltpu.get_barrier_semaphore()
    for device in around:
        pl.semaphore_signal(barrier, inc=1, device_id=device, device_id_type=MESH)
    pl.semaphore_wait(barrier, len(around))

    def send(src, dst, s_sem, r_sem, device):
        copy = pltpu.make_async_remote_copy(
            src_ref=src, dst_ref=dst, send_sem=s_sem, recv_sem=r_sem,
            device_id=device, device_id_type=MESH,
        )
        copy.start()
        return copy

    bands = ((2, mid // 2), (2 + mid // 2, mid // 2), (0, 2), (cy - 2, 2))
    for group in faces:
        loaded(*group)
    x_sends = []
    for b, (y0, ny) in enumerate(bands):
        rows = pl.ds(y0 + 2, ny)
        x_sends.append((
            send(u.at[:, pl.ds(cx, 2), rows], u.at[:, pl.ds(0, 2), rows],
                 xs_sem.at[0, b], xr_sem.at[0, b], (d_next, tile)),
            send(u.at[:, pl.ds(2, 2), rows], u.at[:, pl.ds(cx + 2, 2), rows],
                 xs_sem.at[1, b], xr_sem.at[1, b], (d_prev, tile)),
        ))
    for group in edges:
        loaded(*group)
    own_x = pl.ds(2, cx)
    y_sends = (
        send(u.at[:, own_x, pl.ds(cy, 2)], u.at[:, own_x, pl.ds(0, 2)],
             ys_sem.at[0], yr_sem.at[0], (depth, t_next)),
        send(u.at[:, own_x, pl.ds(2, 2)], u.at[:, own_x, pl.ds(cy + 2, 2)],
             ys_sem.at[1], yr_sem.at[1], (depth, t_prev)),
    )
    loaded(*middle)

    position = lax.broadcasted_iota(jnp.int32, (CHUNKS, CHUNKS), 0)
    wanted = 2 * lax.rem(position, HALF) + position // HALF
    pick = lax.broadcasted_iota(jnp.int32, (CHUNKS, CHUNKS), 1) == wanted
    half_peak = 0.5 * ALPHA_PEAK
    for bx in range(cx // 8):
        rows_of = bricks[bx]
        for by in range(cy // 4):
            line = rows_of[by : by + 1].astype(jnp.float32) * half_peak
            column = jnp.sum(
                jnp.where(pick, jnp.broadcast_to(line, (CHUNKS, CHUNKS)), 0.0),
                axis=1, keepdims=True,
            )
            flags[bx, by] = jnp.broadcast_to(column, (CHUNKS, LANES))

    big = 4
    def inside(step, carry):
        q_rows(u, q, 2 + step // (mid // big), 2 + big * lax.rem(step, mid // big), big)
        return carry

    lax.fori_loop(0, inner * (mid // big), inside, 0)

    def face_x(i):
        return i + jnp.where(i >= 2, cx - 4, 0)

    q_sends = []
    for b in range(2):
        y0, ny = bands[b]
        for copy in x_sends[b]:
            copy.wait_recv()

        @pl.when(depth == 0)
        def _(y0=y0, ny=ny):
            u[:, 0:2, y0 + 2 : y0 + 2 + ny] = jnp.zeros((3, 2, ny, CHUNKS, LANES), jnp.float32)

        @pl.when(depth == nd - 1)
        def _(y0=y0, ny=ny):
            u[:, cx + 2 : cx + 4, y0 + 2 : y0 + 2 + ny] = jnp.zeros(
                (3, 2, ny, CHUNKS, LANES), jnp.float32)

        def outside(step, carry, y0=y0, ny=ny):
            q_rows(u, q, face_x(step // (ny // 2)), y0 + 2 * lax.rem(step, ny // 2), 2)
            return carry

        lax.fori_loop(0, 4 * (ny // 2), outside, 0)
        rows = pl.ds(y0 + 1, ny)
        q_sends.append(send(q.at[cx, rows], q.at[0, rows],
                            qs_sem.at[len(q_sends)], qr_sem.at[len(q_sends)], (d_next, tile)))
        q_sends.append(send(q.at[1, rows], q.at[cx + 1, rows],
                            qs_sem.at[len(q_sends)], qr_sem.at[len(q_sends)], (d_prev, tile)))

    for b in (2, 3):
        for copy in x_sends[b]:
            copy.wait_recv()
    for copy in y_sends:
        copy.wait_recv()

    for b in (2, 3):
        y0 = bands[b][0]

        @pl.when(depth == 0)
        def _(y0=y0):
            u[:, 0:2, y0 + 2 : y0 + 4] = jnp.zeros((3, 2, 2, CHUNKS, LANES), jnp.float32)

        @pl.when(depth == nd - 1)
        def _(y0=y0):
            u[:, cx + 2 : cx + 4, y0 + 2 : y0 + 4] = jnp.zeros((3, 2, 2, CHUNKS, LANES), jnp.float32)

    @pl.when(tile == 0)
    def _():
        u[:, 2 : cx + 2, 0:2] = jnp.zeros((3, cx, 2, CHUNKS, LANES), jnp.float32)

    @pl.when(tile == nt - 1)
    def _():
        u[:, 2 : cx + 2, cy + 2 : cy + 4] = jnp.zeros((3, cx, 2, CHUNKS, LANES), jnp.float32)

    def rim(step, carry):
        q_rows(u, q, step // 2, (cy - 2) * lax.rem(step, 2), 2)
        return carry

    lax.fori_loop(0, 2 * cx, rim, 0)
    own_q = pl.ds(1, cx)
    last = (
        (q.at[own_q, cy], q.at[own_q, 0], (depth, t_next)),
        (q.at[own_q, 1], q.at[own_q, cy + 1], (depth, t_prev)),
        (q.at[cx, pl.ds(1, 2)], q.at[0, pl.ds(1, 2)], (d_next, tile)),
        (q.at[1, pl.ds(1, 2)], q.at[cx + 1, pl.ds(1, 2)], (d_prev, tile)),
        (q.at[cx, pl.ds(cy - 1, 2)], q.at[0, pl.ds(cy - 1, 2)], (d_next, tile)),
        (q.at[1, pl.ds(cy - 1, 2)], q.at[cx + 1, pl.ds(cy - 1, 2)], (d_prev, tile)),
        (q.at[cx, cy], q.at[0, 0], (d_next, t_next)),
        (q.at[cx, 1], q.at[0, cy + 1], (d_next, t_prev)),
        (q.at[1, cy], q.at[cx + 1, 0], (d_prev, t_next)),
        (q.at[1, 1], q.at[cx + 1, cy + 1], (d_prev, t_prev)),
    )
    for src, dst, device in last:
        k = len(q_sends)
        q_sends.append(send(src, dst, qs_sem.at[k], qr_sem.at[k], device))
    for copy in q_sends:
        copy.wait_recv()

    @pl.when(depth == 0)
    def _():
        q[0] = jnp.zeros((cy + 2, CHUNKS, LANES), jnp.float32)

    @pl.when(depth == nd - 1)
    def _():
        q[cx + 1] = jnp.zeros((cy + 2, CHUNKS, LANES), jnp.float32)

    @pl.when(tile == 0)
    def _():
        q[:, 0] = jnp.zeros((cx + 2, CHUNKS, LANES), jnp.float32)

    @pl.when(tile == nt - 1)
    def _():
        q[:, cy + 1] = jnp.zeros((cx + 2, CHUNKS, LANES), jnp.float32)

    flip = sign[0]
    scale = -1.0 / (288.0 * 64.0)

    def rows_pair(pair, carry):
        y = 2 * pair

        def along(view):
            return view + flip * (cx - 1 - 2 * view)

        def y_blurred(x):
            span = q[x + 1, pl.ds(y, 4)]
            return (span[0:2] + span[2:4]) + 2.0 * span[1:3]

        def layer(view, state):
            before, here, trans, sum_a, sum_b, sum_c = state
            x = along(view)
            after = y_blurred(along(view + 1))
            smooth = z_blur((before + after) + 2.0 * here)
            v0 = u[0, x + 2, pl.ds(y + 2, 2)]
            v1 = u[1, x + 2, pl.ds(y + 2, 2)]
            v2 = u[2, x + 2, pl.ds(y + 2, 2)]
            speed = v0 * v0 + v1 * v1 + v2 * v2
            peak = flags[x // 8, y // 4][None]
            tanh_q = jnp.tanh(scale * smooth)
            tanh_half = jnp.tanh((0.5 * scale) * smooth)
            tanh_speed = jnp.tanh(0.5 * speed - 1.5)
            weight = trans * (peak + peak * tanh_q)
            return (here, after, trans - weight, sum_a + weight * tanh_half,
                    sum_b + weight * tanh_speed, sum_c + weight * tanh_q)

        one = jnp.ones((2, CHUNKS, LANES), jnp.float32)
        zero = jnp.zeros((2, CHUNKS, LANES), jnp.float32)
        state = (y_blurred(along(-1)), y_blurred(along(0)), one, zero, zero, zero)
        state = lax.fori_loop(0, cx, layer, state, unroll=2)
        _, _, trans, sum_a, sum_b, sum_c = state
        covered = 1.0 - trans
        rows = pl.ds(y, 2)
        image[0, rows] = trans
        image[1, rows] = 0.5 * (covered + sum_a)
        image[2, rows] = 0.5 * (covered + sum_b)
        image[3, rows] = 0.5 * (covered - sum_c)
        return carry

    lax.fori_loop(0, cy // 2, rows_pair, 0)

    def piece(d, par, where):
        return image.at[:, :, HALF * par + d], pieces.at[where, :, :, pl.ds(par * LANES, LANES)]

    for d in range(nd):
        for par in range(2):
            src, dst = piece(d, par, depth)

            @pl.when(depth != d)
            def _(src=src, dst=dst, d=d, par=par):
                send(src, dst, is_sem.at[d, par], ir_sem.at[depth, par], (d, tile))

            @pl.when(depth == d)
            def _(src=src, dst=dst, par=par):
                pltpu.make_async_copy(src, dst, own_sem.at[par]).start()

    for d in range(nd):
        for par in range(2):
            src, dst = piece(d, par, d)

            @pl.when(depth != d)
            def _(src=src, dst=dst, d=d, par=par):
                copy = pltpu.make_async_remote_copy(
                    src_ref=src, dst_ref=dst, send_sem=is_sem.at[d, par],
                    recv_sem=ir_sem.at[d, par], device_id=(d, tile), device_id_type=MESH)
                copy.wait()

            @pl.when(depth == d)
            def _(src=src, dst=dst, par=par):
                pltpu.make_async_copy(src, dst, own_sem.at[par]).wait()

    total = None
    for view in range(nd):
        part = pieces[view + flip * (nd - 1 - 2 * view)]
        if total is None:
            trans, shade = part[0], part[1:]
        else:
            shade = shade + trans[None] * part[1:]
            trans = trans * part[0]
        total = view
    color[...] = shade
    alpha[...] = 1.0 - trans

    for pair in x_sends:
        for copy in pair:
            copy.wait_send()
    for copy in y_sends:
        copy.wait_send()
    for copy in q_sends:
        copy.wait_send()


def solution(mesh):
    nd, nt = mesh.shape["depth"], mesh.shape["tile"]

    def per_device(velocity, view_sign, brick_flags):
        _, cx, cy, cz = velocity.shape
        width = cz // nd
        dma = pltpu.SemaphoreType.DMA

        def body(*refs):
            kernel(nd, nt, cx, cy, *refs)

        return pl.pallas_call(
            body,
            out_shape=(
                jax.ShapeDtypeStruct((3, cy, width), jnp.float32),
                jax.ShapeDtypeStruct((cy, width), jnp.float32),
            ),
            in_specs=[
                pl.BlockSpec(memory_space=pl.ANY),
                pl.BlockSpec(memory_space=pltpu.SMEM),
                pl.BlockSpec(memory_space=pltpu.VMEM),
            ],
            out_specs=(
                pl.BlockSpec(memory_space=pltpu.VMEM),
                pl.BlockSpec(memory_space=pltpu.VMEM),
            ),
            scratch_shapes=[
                pltpu.VMEM((3, cx + 4, cy + 4, CHUNKS, LANES), jnp.float32),
                pltpu.VMEM((cx + 2, cy + 2, CHUNKS, LANES), jnp.float32),
                pltpu.VMEM((cx // 8, cy // 4, CHUNKS, LANES), jnp.float32),
                pltpu.VMEM((4, cy, CHUNKS, LANES), jnp.float32),
                pltpu.VMEM((nd, 4, cy, width), jnp.float32),
                dma((5,)),
                dma((2, 4)), dma((2, 4)), dma((2,)), dma((2,)),
                dma((14,)), dma((14,)), dma((nd, 2)), dma((nd, 2)), dma((2,)),
            ],
            compiler_params=pltpu.CompilerParams(
                collective_id=0, has_side_effects=True, vmem_limit_bytes=56 << 20
            ),
        )(velocity, view_sign, brick_flags)

    placed = (P(None, "depth", "tile", None), P("tile"), P("depth", "tile", None))
    return jax.shard_map(
        per_device,
        mesh=mesh,
        in_specs=placed,
        out_specs=(P(None, "tile", "depth"), P("tile", "depth")),
        check_vma=False,
    )
```

time: 304 us -> 78.9 us (0.26)
  the two profiles are of different devices: /device:TPU:96 before, /device:TPU:1 now
where the time goes in v1:
time: 78.9 us; the launch traced here: 78.7 us
  Pallas kernels  74.5 us (94%)
  local copies, waits for them, and re-layouts  2.91 us (4%)
  between operations  1.28 us (2%)
    pallas_call x1, Pallas kernels, per_device(): pl.pallas_call(body, out_shape=(jax.ShapeDtypeStruct((3, cy, width), jnp....  74.5 us
    unnamed x2, local copies, waits for them, and re-layouts  2.91 us

profile of v1, /device:TPU:1, one launch (start us, length us, event | category | flops | bytes accessed | tf_op | source)
XLA Modules:
  0.0 78.7 jit_solution(17312051476000227424)
XLA Ops:
  1.3 74.5 %shard_map.50 = (f32[3,32,256]{2,1,0:T(8,128)}, f32[32,256]{1,0:T(8,128)}) custom-call(f32[3,16,32,2048]{3,2,1,0:T(8,128)} %refs_0_.1, s32[1]{0:T(128)S(6)} %copy.7.refs_1_, s32[2,8,16]{2,1,0:T(8,128)} %refs_2_.1), custom_call_target="tpu_custom_call" | custom-call | tf_op jit(solution)/shard_map/pallas_call | solution.py:363
  75.7 1.5 %copy.8 = f32[3,32,256]{2,1,0:T(8,128)} copy(f32[3,32,256]{2,1,0:T(8,128)} %get-tuple-element.4) | data formatting | bytes 196608
  77.3 1.4 %copy.9 = f32[32,256]{1,0:T(8,128)} copy(f32[32,256]{1,0:T(8,128)} %get-tuple-element.5) | data formatting | bytes 65536

commit v2 on v1

v2 whole, which is shorter than its diff:
```python
import jax
import jax.numpy as jnp
from jax import lax
from jax.experimental import pallas as pl
from jax.experimental.pallas import tpu as pltpu
from jax.sharding import PartitionSpec as P

ALPHA_PEAK = 0.04
MESH = pl.DeviceIdType.MESH
LANES = 128
HALF = 8
CHUNKS = 2 * HALF


def split(value):
    high = value.astype(jnp.bfloat16)
    return high, (value - high.astype(jnp.float32)).astype(jnp.bfloat16)


def band_matrix(taps):
    shape = (6 * LANES, 2 * LANES)
    row = lax.broadcasted_iota(jnp.int32, shape, 0)
    lane = lax.rem(row, LANES)
    apart = jnp.where(lane < LANES // 2, lane + 2 * LANES, lane - LANES)
    cell = jnp.where(row < 4 * LANES, lax.rem(row, 2 * LANES), apart)
    offset = cell - lax.broadcasted_iota(jnp.int32, shape, 1)
    band = jnp.zeros(shape, jnp.float32)
    for at, weight in taps:
        band = jnp.where(offset == at, weight, band)
    return band.astype(jnp.bfloat16)


def along_z(value, band):
    lead = value.shape[:-2]
    flat = value.reshape((-1, CHUNKS, LANES))
    even, odd = flat[:, :HALF], flat[:, HALF:]
    lane = lax.broadcasted_iota(jnp.int32, even.shape, 2)
    sub = lax.broadcasted_iota(jnp.int32, even.shape, 1)
    beside = jnp.where(lane < 2, pltpu.roll(even, HALF - 1, 1), pltpu.roll(odd, 1, 1))
    outside = ((lane < 2) & (sub == HALF - 1)) | ((lane >= 2) & (sub == 0))
    beside = jnp.where(outside, 0.0, beside)
    parts = [split(v.reshape((-1, LANES))) for v in (even, odd, beside)]
    (e_hi, e_lo), (o_hi, o_lo), (b_hi, b_lo) = parts
    operand = jnp.concatenate([e_hi, o_hi, e_lo, o_lo, b_hi, b_lo], axis=1)
    out = jnp.dot(operand, band[...], preferred_element_type=jnp.float32)
    halves = [out[:, h * LANES : (h + 1) * LANES].reshape((-1, HALF, LANES)) for h in range(2)]
    return jnp.concatenate(halves, axis=1).reshape(lead + (CHUNKS, LANES))


def q_rows(u, gz, q, x, y, rows):
    def parts(comp):
        span = u[comp, x + 2, pl.ds(y, rows + 4)]
        near_x = u[comp, x + 3, pl.ds(y + 2, rows)] - u[comp, x + 1, pl.ds(y + 2, rows)]
        far_x = u[comp, x + 4, pl.ds(y + 2, rows)] - u[comp, x, pl.ds(y + 2, rows)]
        near_y = span[3 : rows + 3] - span[1 : rows + 1]
        far_y = span[4:] - span[:rows]
        return (
            8.0 * near_x - far_x,
            8.0 * near_y - far_y,
            gz[comp, x, pl.ds(y, rows)],
        )

    g00, g01, g02 = parts(0)
    total = g00 * g00
    g10, g11, g12 = parts(1)
    total = total + g11 * g11
    cross = g01 * g10
    g20, g21, g22 = parts(2)
    total = total + g22 * g22
    cross = cross + g02 * g20 + g12 * g21
    q[x, pl.ds(y, rows)] = total + (cross + cross)


def kernel(
    nd, nt, cx, cy, vel, sign, bricks, color, alpha,
    u, gz, raw, q, q_low, q_high, slope, smoother, flags, image, pieces, load_sem,
    xs_sem, xr_sem, ys_sem, yr_sem, qs_sem, qr_sem, is_sem, ir_sem, own_sem,
):
    depth, tile = lax.axis_index("depth"), lax.axis_index("tile")
    d_next, d_prev = lax.rem(depth + 1, nd), lax.rem(depth + nd - 1, nd)
    t_next, t_prev = lax.rem(tile + 1, nt), lax.rem(tile + nt - 1, nt)
    inner = cx - 4
    mid = cy - 4

    def load(group, x0, nx, y0, ny):
        for comp in range(3):
            for chunk in range(CHUNKS):
                pltpu.make_async_copy(
                    vel.at[comp, pl.ds(x0, nx), pl.ds(y0, ny), pl.ds(chunk * LANES, LANES)],
                    u.at[comp, pl.ds(x0 + 2, nx), pl.ds(y0 + 2, ny),
                         HALF * (chunk % 2) + chunk // 2],
                    load_sem.at[group],
                ).start()

    def loaded(group, x0, nx, y0, ny):
        where = u.at[:, pl.ds(x0 + 2, nx), pl.ds(y0 + 2, ny)]
        pltpu.make_async_copy(where, where, load_sem.at[group]).wait()

    faces = ((0, cx - 2, 2, 0, cy), (1, 0, 2, 0, cy))
    edges = ((2, 2, inner, 0, 8), (3, 2, inner, cy - 8, 8))
    middle = (4, 2, inner, 8, cy - 16)
    for group in faces + edges + (middle,):
        load(*group)

    around = [(d_next, tile), (d_prev, tile), (depth, t_next), (depth, t_prev),
              (d_next, t_next), (d_next, t_prev), (d_prev, t_next), (d_prev, t_prev)]
    around += [(lax.rem(depth + hop, nd), tile) for hop in range(2, nd - 1)]
    barrier = pltpu.get_barrier_semaphore()
    for device in around:
        pl.semaphore_signal(barrier, inc=1, device_id=device, device_id_type=MESH)
    pl.semaphore_wait(barrier, len(around))

    def send(src, dst, s_sem, r_sem, device):
        copy = pltpu.make_async_remote_copy(
            src_ref=src, dst_ref=dst, send_sem=s_sem, recv_sem=r_sem,
            device_id=device, device_id_type=MESH,
        )
        copy.start()
        return copy

    first = mid // 8 * 4
    bands = ((2, first), (2 + first, mid - first), (0, 2), (cy - 2, 2))
    for group in faces:
        loaded(*group)
    x_sends = []
    for b, (y0, ny) in enumerate(bands):
        rows = pl.ds(y0 + 2, ny)
        x_sends.append((
            send(u.at[:, pl.ds(cx, 2), rows], u.at[:, pl.ds(0, 2), rows],
                 xs_sem.at[0, b], xr_sem.at[0, b], (d_next, tile)),
            send(u.at[:, pl.ds(2, 2), rows], u.at[:, pl.ds(cx + 2, 2), rows],
                 xs_sem.at[1, b], xr_sem.at[1, b], (d_prev, tile)),
        ))
    for group in edges:
        loaded(*group)
    own_x = pl.ds(2, cx)
    y_sends = (
        send(u.at[:, own_x, pl.ds(cy, 2)], u.at[:, own_x, pl.ds(0, 2)],
             ys_sem.at[0], yr_sem.at[0], (depth, t_next)),
        send(u.at[:, own_x, pl.ds(2, 2)], u.at[:, own_x, pl.ds(cy + 2, 2)],
             ys_sem.at[1], yr_sem.at[1], (depth, t_prev)),
    )
    loaded(*middle)

    position = lax.broadcasted_iota(jnp.int32, (CHUNKS, CHUNKS), 0)
    wanted = 2 * lax.rem(position, HALF) + position // HALF
    pick = lax.broadcasted_iota(jnp.int32, (CHUNKS, CHUNKS), 1) == wanted
    half_peak = 0.5 * ALPHA_PEAK
    for bx in range(cx // 8):
        rows_of = bricks[bx]
        for by in range(cy // 4):
            line = rows_of[by : by + 1].astype(jnp.float32) * half_peak
            column = jnp.sum(
                jnp.where(pick, jnp.broadcast_to(line, (CHUNKS, CHUNKS)), 0.0),
                axis=1, keepdims=True,
            )
            flags[bx, by] = jnp.broadcast_to(column, (CHUNKS, LANES))

    slope[...] = band_matrix(((-2, 1.0), (-1, -8.0), (1, 8.0), (2, -1.0)))
    smoother[...] = band_matrix(((-1, 1.0), (0, 2.0), (1, 1.0)))
    own_y = pl.ds(2, cy)

    def z_plane(x, carry):
        for comp in range(3):
            gz[comp, x] = along_z(u[comp, x + 2, own_y], slope)
        return carry

    lax.fori_loop(0, cx, z_plane, 0)

    big = 4

    def inside(step, carry):
        x = step + 2

        def block(k, carry):
            q_rows(u, gz, raw, x, 2 + big * k, big)
            return carry

        lax.fori_loop(0, mid // big, block, 0)
        q[x + 1] = along_z(raw[x, pl.ds(2, mid)], smoother)
        return carry

    lax.fori_loop(0, inner, inside, 0)

    def face_x(i):
        return i + jnp.where(i >= 2, cx - 4, 0)

    q_sends = []

    def send_q(src, dst, device):
        k = len(q_sends)
        q_sends.append(send(src, dst, qs_sem.at[k], qr_sem.at[k], device))

    for b in range(2):
        y0, ny = bands[b]
        for copy in x_sends[b]:
            copy.wait_recv()

        @pl.when(depth == 0)
        def _(y0=y0, ny=ny):
            u[:, 0:2, y0 + 2 : y0 + 2 + ny] = jnp.zeros((3, 2, ny, CHUNKS, LANES), jnp.float32)

        @pl.when(depth == nd - 1)
        def _(y0=y0, ny=ny):
            u[:, cx + 2 : cx + 4, y0 + 2 : y0 + 2 + ny] = jnp.zeros(
                (3, 2, ny, CHUNKS, LANES), jnp.float32)

        def outside(step, carry, y0=y0, ny=ny):
            q_rows(u, gz, raw, face_x(step // (ny // big)), y0 + big * lax.rem(step, ny // big), big)
            return carry

        lax.fori_loop(0, 4 * (ny // big), outside, 0)
        rows = pl.ds(y0 - 2, ny)
        for x0 in (0, cx - 2):
            q[pl.ds(x0 + 1, 2), rows] = along_z(raw[pl.ds(x0, 2), pl.ds(y0, ny)], smoother)
        send_q(q.at[cx, rows], q.at[0, rows], (d_next, tile))
        send_q(q.at[1, rows], q.at[cx + 1, rows], (d_prev, tile))

    for b in (2, 3):
        for copy in x_sends[b]:
            copy.wait_recv()
    for copy in y_sends:
        copy.wait_recv()

    for b in (2, 3):
        y0 = bands[b][0]

        @pl.when(depth == 0)
        def _(y0=y0):
            u[:, 0:2, y0 + 2 : y0 + 4] = jnp.zeros((3, 2, 2, CHUNKS, LANES), jnp.float32)

        @pl.when(depth == nd - 1)
        def _(y0=y0):
            u[:, cx + 2 : cx + 4, y0 + 2 : y0 + 4] = jnp.zeros((3, 2, 2, CHUNKS, LANES), jnp.float32)

    @pl.when(tile == 0)
    def _():
        u[:, 2 : cx + 2, 0:2] = jnp.zeros((3, cx, 2, CHUNKS, LANES), jnp.float32)

    @pl.when(tile == nt - 1)
    def _():
        u[:, 2 : cx + 2, cy + 2 : cy + 4] = jnp.zeros((3, cx, 2, CHUNKS, LANES), jnp.float32)

    def rim(x, carry):
        q_rows(u, gz, raw, x, 0, 2)
        q_rows(u, gz, raw, x, cy - 2, 2)
        return carry

    lax.fori_loop(0, cx, rim, 0)
    own_q = pl.ds(1, cx)
    q_low[own_q, 1:3] = along_z(raw[:, 0:2], smoother)
    q_high[own_q, 0:2] = along_z(raw[:, cy - 2 : cy], smoother)
    inner_sends = len(q_sends)
    send_q(q_high.at[own_q, 1], q_low.at[own_q, 0], (depth, t_next))
    send_q(q_low.at[own_q, 1], q_high.at[own_q, 2], (depth, t_prev))
    for part, rows in ((q_low, pl.ds(1, 2)), (q_high, pl.ds(0, 2))):
        send_q(part.at[cx, rows], part.at[0, rows], (d_next, tile))
        send_q(part.at[1, rows], part.at[cx + 1, rows], (d_prev, tile))
    send_q(q_high.at[cx, 1], q_low.at[0, 0], (d_next, t_next))
    send_q(q_low.at[cx, 1], q_high.at[0, 2], (d_next, t_prev))
    send_q(q_high.at[1, 1], q_low.at[cx + 1, 0], (d_prev, t_next))
    send_q(q_low.at[1, 1], q_high.at[cx + 1, 2], (d_prev, t_prev))

    for copy in q_sends[:inner_sends]:
        copy.wait_recv()

    @pl.when(depth == 0)
    def _():
        q[0] = jnp.zeros((mid, CHUNKS, LANES), jnp.float32)

    @pl.when(depth == nd - 1)
    def _():
        q[cx + 1] = jnp.zeros((mid, CHUNKS, LANES), jnp.float32)

    flip = sign[0]
    scale = -1.0 / (288.0 * 64.0)

    def along(view):
        return view + flip * (cx - 1 - 2 * view)

    def composite(y, rows, span_of, unroll):
        def y_blurred(x):
            span = span_of(x)
            return (span[0:rows] + span[2 : rows + 2]) + 2.0 * span[1 : rows + 1]

        def layer(view, state):
            before, here, trans, sum_a, sum_b, sum_c = state
            x = along(view)
            after = y_blurred(along(view + 1))
            smooth = (before + after) + 2.0 * here
            v0 = u[0, x + 2, pl.ds(y + 2, rows)]
            v1 = u[1, x + 2, pl.ds(y + 2, rows)]
            v2 = u[2, x + 2, pl.ds(y + 2, rows)]
            speed = v0 * v0 + v1 * v1 + v2 * v2
            peak = flags[x // 8, y // 4][None]
            tanh_q = jnp.tanh(scale * smooth)
            tanh_half = jnp.tanh((0.5 * scale) * smooth)
            tanh_speed = jnp.tanh(0.5 * speed - 1.5)
            weight = trans * (peak + peak * tanh_q)
            return (here, after, trans - weight, sum_a + weight * tanh_half,
                    sum_b + weight * tanh_speed, sum_c + weight * tanh_q)

        one = jnp.ones((rows, CHUNKS, LANES), jnp.float32)
        zero = jnp.zeros((rows, CHUNKS, LANES), jnp.float32)
        state = (y_blurred(along(-1)), y_blurred(along(0)), one, zero, zero, zero)
        state = lax.fori_loop(0, cx, layer, state, unroll=unroll)
        _, _, trans, sum_a, sum_b, sum_c = state
        covered = 1.0 - trans
        where = pl.ds(y, rows)
        image[0, where] = trans
        image[1, where] = 0.5 * (covered + sum_a)
        image[2, where] = 0.5 * (covered + sum_b)
        image[3, where] = 0.5 * (covered - sum_c)

    def middle_rows(y0, count):
        def pair(k, carry):
            y = y0 + 2 * k
            composite(y, 2, lambda x: q[x + 1, pl.ds(y - 3, 4)], 4)
            return carry

        lax.fori_loop(0, count // 2, pair, 0)

    def piece(d, par, where, group):
        rows = pl.ds(8 * group, 8)
        return image.at[:, rows, HALF * par + d], pieces.at[where, :, par, rows]

    def send_image(group):
        for hop in range(1, nd):
            for d in range(nd):
                @pl.when(d == lax.rem(depth + hop, nd))
                def _(d=d):
                    for par in range(2):
                        src, dst = piece(d, par, depth, group)
                        send(src, dst, is_sem.at[group, d, par], ir_sem.at[group, depth, par], (d, tile))
        for d in range(nd):
            @pl.when(depth == d)
            def _(d=d):
                for par in range(2):
                    src, dst = piece(d, par, depth, group)
                    pltpu.make_async_copy(src, dst, own_sem.at[group, par]).start()

    groups = cy // 8
    for group in range(1, groups - 1):
        middle_rows(8 * group, 8)
        send_image(group)
    middle_rows(4, 4)
    middle_rows(cy - 8, 4)

    for copy in q_sends[inner_sends:]:
        copy.wait_recv()

    @pl.when(depth == 0)
    def _():
        q_low[0] = jnp.zeros((3, CHUNKS, LANES), jnp.float32)
        q_high[0] = jnp.zeros((3, CHUNKS, LANES), jnp.float32)

    @pl.when(depth == nd - 1)
    def _():
        q_low[cx + 1] = jnp.zeros((3, CHUNKS, LANES), jnp.float32)
        q_high[cx + 1] = jnp.zeros((3, CHUNKS, LANES), jnp.float32)

    @pl.when(tile == 0)
    def _():
        q_low[:, 0] = jnp.zeros((cx + 2, CHUNKS, LANES), jnp.float32)

    @pl.when(tile == nt - 1)
    def _():
        q_high[:, 2] = jnp.zeros((cx + 2, CHUNKS, LANES), jnp.float32)

    composite(0, 4, lambda x: jnp.concatenate([q_low[x + 1], q[x + 1, 0:3]], axis=0), 2)
    send_image(0)
    composite(cy - 4, 4, lambda x: jnp.concatenate(
        [q[x + 1, mid - 3 : mid], q_high[x + 1]], axis=0), 2)
    send_image(groups - 1)

    for group in list(range(1, groups - 1)) + [0, groups - 1]:
        for d in range(nd):
            @pl.when(depth != d)
            def _(d=d, group=group):
                for par in range(2):
                    src, _ = piece(d, par, depth, group)
                    _, dst = piece(d, par, d, group)
                    pltpu.make_async_remote_copy(
                        src_ref=src, dst_ref=dst, send_sem=is_sem.at[group, d, par],
                        recv_sem=ir_sem.at[group, d, par], device_id=(d, tile),
                        device_id_type=MESH).wait()

            @pl.when(depth == d)
            def _(d=d, group=group):
                for par in range(2):
                    src, dst = piece(d, par, d, group)
                    pltpu.make_async_copy(src, dst, own_sem.at[group, par]).wait()

    total = None
    for view in range(nd):
        part = pieces[view + flip * (nd - 1 - 2 * view)]
        if total is None:
            trans, shade = part[0], part[1:]
        else:
            shade = shade + trans[None] * part[1:]
            trans = trans * part[0]
        total = view
    for par in range(2):
        lanes = slice(par * LANES, (par + 1) * LANES)
        color[:, :, lanes] = shade[:, par]
        alpha[:, lanes] = 1.0 - trans[par]

    for pair in x_sends:
        for copy in pair:
            copy.wait_send()
    for copy in y_sends:
        copy.wait_send()
    for copy in q_sends:
        copy.wait_send()


def solution(mesh):
    nd, nt = mesh.shape["depth"], mesh.shape["tile"]

    def per_device(velocity, view_sign, brick_flags):
        _, cx, cy, cz = velocity.shape
        width = cz // nd
        dma = pltpu.SemaphoreType.DMA

        def body(*refs):
            kernel(nd, nt, cx, cy, *refs)

        return pl.pallas_call(
            body,
            out_shape=(
                jax.ShapeDtypeStruct((3, cy, width), jnp.float32),
                jax.ShapeDtypeStruct((cy, width), jnp.float32),
            ),
            in_specs=[
                pl.BlockSpec(memory_space=pl.ANY),
                pl.BlockSpec(memory_space=pltpu.SMEM),
                pl.BlockSpec(memory_space=pltpu.VMEM),
            ],
            out_specs=(
                pl.BlockSpec(memory_space=pltpu.VMEM),
                pl.BlockSpec(memory_space=pltpu.VMEM),
            ),
            scratch_shapes=[
                pltpu.VMEM((3, cx + 4, cy + 4, CHUNKS, LANES), jnp.float32),
                pltpu.VMEM((3, cx, cy, CHUNKS, LANES), jnp.float32),
                pltpu.VMEM((cx, cy, CHUNKS, LANES), jnp.float32),
                pltpu.VMEM((cx + 2, cy - 4, CHUNKS, LANES), jnp.float32),
                pltpu.VMEM((cx + 2, 3, CHUNKS, LANES), jnp.float32),
                pltpu.VMEM((cx + 2, 3, CHUNKS, LANES), jnp.float32),
                pltpu.VMEM((6 * LANES, 2 * LANES), jnp.bfloat16),
                pltpu.VMEM((6 * LANES, 2 * LANES), jnp.bfloat16),
                pltpu.VMEM((cx // 8, cy // 4, CHUNKS, LANES), jnp.float32),
                pltpu.VMEM((4, cy, CHUNKS, LANES), jnp.float32),
                pltpu.VMEM((nd, 4, 2, cy, width // 2), jnp.float32),
                dma((5,)),
                dma((2, 4)), dma((2, 4)), dma((2,)), dma((2,)),
                dma((14,)), dma((14,)), dma((cy // 8, nd, 2)), dma((cy // 8, nd, 2)), dma((cy // 8, 2)),
            ],
            compiler_params=pltpu.CompilerParams(
                collective_id=0, has_side_effects=True, vmem_limit_bytes=56 << 20
            ),
        )(velocity, view_sign, brick_flags)

    placed = (P(None, "depth", "tile", None), P("tile"), P("depth", "tile", None))
    return jax.shard_map(
        per_device,
        mesh=mesh,
        in_specs=placed,
        out_specs=(P(None, "tile", "depth"), P("tile", "depth")),
        check_vma=False,
    )
```

time: 78.9 us -> 55.5 us (0.70)
  Pallas kernels: 74.5 us -> 51 us
    pallas_call x1, Pallas kernels: 74.5 us -> 51 us  [per_device(): pl.pallas_call(body, out_shape=(jax.ShapeDtypeStruct((3, cy, width), jnp....]
where the time goes in v2:
time: 55.5 us; the launch traced here: 55.2 us
  Pallas kernels  51 us (92%)
  local copies, waits for them, and re-layouts  2.91 us (5%)
  between operations  1.28 us (2%)
    pallas_call x1, Pallas kernels, per_device(): pl.pallas_call(body, out_shape=(jax.ShapeDtypeStruct((3, cy, width), jnp....  51 us
    unnamed x2, local copies, waits for them, and re-layouts  2.91 us

profile of v2, /device:TPU:1, one launch (start us, length us, event | category | flops | bytes accessed | tf_op | source)
XLA Modules:
  0.0 55.2 jit_solution(15929295481662332312)
XLA Ops:
  1.3 51.0 %shard_map.50 = (f32[3,32,256]{2,1,0:T(8,128)}, f32[32,256]{1,0:T(8,128)}) custom-call(f32[3,16,32,2048]{3,2,1,0:T(8,128)} %refs_0_.1, s32[1]{0:T(128)S(6)} %copy.7.refs_1_, s32[2,8,16]{2,1,0:T(8,128)} %refs_2_.1), custom_call_target="tpu_custom_call" | custom-call | tf_op jit(solution)/shard_map/pallas_call | solution.py:428
  52.3 1.5 %copy.8 = f32[3,32,256]{2,1,0:T(8,128)} copy(f32[3,32,256]{2,1,0:T(8,128)} %get-tuple-element.4) | data formatting | bytes 196608
  53.8 1.4 %copy.9 = f32[32,256]{1,0:T(8,128)} copy(f32[32,256]{1,0:T(8,128)} %get-tuple-element.5) | data formatting | bytes 65536

commit v3 on v2

--- a/solution.py
+++ b/solution.py
@@ -72,9 +72,9 @@
 
 
 def kernel(
-    nd, nt, cx, cy, vel, sign, bricks, color, alpha,
-    u, gz, raw, q, q_low, q_high, slope, smoother, flags, image, pieces, load_sem,
-    xs_sem, xr_sem, ys_sem, yr_sem, qs_sem, qr_sem, is_sem, ir_sem, own_sem,
+    nd, nt, cx, cy, vel, sign, bricks, result,
+    u, gz, raw, q, q_low, q_high, slope, smoother, flags, image, near, merged, far, load_sem,
+    xs_sem, xr_sem, ys_sem, yr_sem, qs_sem, qr_sem, is_sem, ir_sem, own_sem, fs_sem, fr_sem,
 ):
     depth, tile = lax.axis_index("depth"), lax.axis_index("tile")
     d_next, d_prev = lax.rem(depth + 1, nd), lax.rem(depth + nd - 1, nd)
@@ -104,7 +104,7 @@
 
     around = [(d_next, tile), (d_prev, tile), (depth, t_next), (depth, t_prev),
               (d_next, t_next), (d_next, t_prev), (d_prev, t_next), (d_prev, t_prev)]
-    around += [(lax.rem(depth + hop, nd), tile) for hop in range(2, nd - 1)]
+    around += [(lax.rem(depth + hop, nd), tile) for hop in range(2, nd, 2)]
     barrier = pltpu.get_barrier_semaphore()
     for device in around:
         pl.semaphore_signal(barrier, inc=1, device_id=device, device_id_type=MESH)
@@ -118,28 +118,37 @@
         copy.start()
         return copy
 
-    first = mid // 8 * 4
-    bands = ((2, first), (2 + first, mid - first), (0, 2), (cy - 2, 2))
+    bands = ((10, cy - 20), (0, 2), (cy - 2, 2), (2, 8), (cy - 10, 8))
     for group in faces:
         loaded(*group)
-    x_sends = []
-    for b, (y0, ny) in enumerate(bands):
+    x_sends, y_sends = {}, {}
+
+    def issue_x(b):
+        y0, ny = bands[b]
         rows = pl.ds(y0 + 2, ny)
-        x_sends.append((
+        x_sends[b] = (
             send(u.at[:, pl.ds(cx, 2), rows], u.at[:, pl.ds(0, 2), rows],
                  xs_sem.at[0, b], xr_sem.at[0, b], (d_next, tile)),
             send(u.at[:, pl.ds(2, 2), rows], u.at[:, pl.ds(cx + 2, 2), rows],
                  xs_sem.at[1, b], xr_sem.at[1, b], (d_prev, tile)),
-        ))
+        )
+
+    half = cx // 2
+
+    def issue_y(h):
+        part_x = pl.ds(2 + h * half, half)
+        y_sends[h] = (
+            send(u.at[:, part_x, pl.ds(cy, 2)], u.at[:, part_x, pl.ds(0, 2)],
+                 ys_sem.at[0, h], yr_sem.at[0, h], (depth, t_next)),
+            send(u.at[:, part_x, pl.ds(2, 2)], u.at[:, part_x, pl.ds(cy + 2, 2)],
+                 ys_sem.at[1, h], yr_sem.at[1, h], (depth, t_prev)),
+        )
+
+    issue_x(0)
+    issue_x(3)
     for group in edges:
         loaded(*group)
-    own_x = pl.ds(2, cx)
-    y_sends = (
-        send(u.at[:, own_x, pl.ds(cy, 2)], u.at[:, own_x, pl.ds(0, 2)],
-             ys_sem.at[0], yr_sem.at[0], (depth, t_next)),
-        send(u.at[:, own_x, pl.ds(2, 2)], u.at[:, own_x, pl.ds(cy + 2, 2)],
-             ys_sem.at[1], yr_sem.at[1], (depth, t_prev)),
-    )
+    issue_y(0)
     loaded(*middle)
 
     position = lax.broadcasted_iota(jnp.int32, (CHUNKS, CHUNKS), 0)
@@ -166,6 +175,9 @@
         return carry
 
     lax.fori_loop(0, cx, z_plane, 0)
+    for b in (1, 2, 4):
+        issue_x(b)
+    issue_y(1)
 
     big = 4
 
@@ -180,88 +192,86 @@
         q[x + 1] = along_z(raw[x, pl.ds(2, mid)], smoother)
         return carry
 
-    lax.fori_loop(0, inner, inside, 0)
-
     def face_x(i):
         return i + jnp.where(i >= 2, cx - 4, 0)
 
-    q_sends = []
-
-    def send_q(src, dst, device):
-        k = len(q_sends)
-        q_sends.append(send(src, dst, qs_sem.at[k], qr_sem.at[k], device))
-
-    for b in range(2):
+    q_sends, rim_sends = [], []
+
+    def send_q(src, dst, device, into):
+        k = len(q_sends) + len(rim_sends)
+        into.append(send(src, dst, qs_sem.at[k], qr_sem.at[k], device))
+
+    def x_arrived(b):
         y0, ny = bands[b]
         for copy in x_sends[b]:
             copy.wait_recv()
 
         @pl.when(depth == 0)
-        def _(y0=y0, ny=ny):
+        def _():
             u[:, 0:2, y0 + 2 : y0 + 2 + ny] = jnp.zeros((3, 2, ny, CHUNKS, LANES), jnp.float32)
 
         @pl.when(depth == nd - 1)
-        def _(y0=y0, ny=ny):
+        def _():
             u[:, cx + 2 : cx + 4, y0 + 2 : y0 + 2 + ny] = jnp.zeros(
                 (3, 2, ny, CHUNKS, LANES), jnp.float32)
 
-        def outside(step, carry, y0=y0, ny=ny):
+    def outside(b):
+        y0, ny = bands[b]
+
+        def block(step, carry):
             q_rows(u, gz, raw, face_x(step // (ny // big)), y0 + big * lax.rem(step, ny // big), big)
             return carry
 
-        lax.fori_loop(0, 4 * (ny // big), outside, 0)
+        lax.fori_loop(0, 4 * (ny // big), block, 0)
         rows = pl.ds(y0 - 2, ny)
         for x0 in (0, cx - 2):
             q[pl.ds(x0 + 1, 2), rows] = along_z(raw[pl.ds(x0, 2), pl.ds(y0, ny)], smoother)
-        send_q(q.at[cx, rows], q.at[0, rows], (d_next, tile))
-        send_q(q.at[1, rows], q.at[cx + 1, rows], (d_prev, tile))
-
-    for b in (2, 3):
-        for copy in x_sends[b]:
+        send_q(q.at[cx, rows], q.at[0, rows], (d_next, tile), q_sends)
+        send_q(q.at[1, rows], q.at[cx + 1, rows], (d_prev, tile), q_sends)
+
+    def rim(h):
+        for copy in y_sends[h]:
             copy.wait_recv()
-    for copy in y_sends:
-        copy.wait_recv()
-
-    for b in (2, 3):
-        y0 = bands[b][0]
-
-        @pl.when(depth == 0)
-        def _(y0=y0):
-            u[:, 0:2, y0 + 2 : y0 + 4] = jnp.zeros((3, 2, 2, CHUNKS, LANES), jnp.float32)
-
-        @pl.when(depth == nd - 1)
-        def _(y0=y0):
-            u[:, cx + 2 : cx + 4, y0 + 2 : y0 + 4] = jnp.zeros((3, 2, 2, CHUNKS, LANES), jnp.float32)
-
-    @pl.when(tile == 0)
-    def _():
-        u[:, 2 : cx + 2, 0:2] = jnp.zeros((3, cx, 2, CHUNKS, LANES), jnp.float32)
-
-    @pl.when(tile == nt - 1)
-    def _():
-        u[:, 2 : cx + 2, cy + 2 : cy + 4] = jnp.zeros((3, cx, 2, CHUNKS, LANES), jnp.float32)
-
-    def rim(x, carry):
-        q_rows(u, gz, raw, x, 0, 2)
-        q_rows(u, gz, raw, x, cy - 2, 2)
-        return carry
-
-    lax.fori_loop(0, cx, rim, 0)
-    own_q = pl.ds(1, cx)
-    q_low[own_q, 1:3] = along_z(raw[:, 0:2], smoother)
-    q_high[own_q, 0:2] = along_z(raw[:, cy - 2 : cy], smoother)
-    inner_sends = len(q_sends)
-    send_q(q_high.at[own_q, 1], q_low.at[own_q, 0], (depth, t_next))
-    send_q(q_low.at[own_q, 1], q_high.at[own_q, 2], (depth, t_prev))
-    for part, rows in ((q_low, pl.ds(1, 2)), (q_high, pl.ds(0, 2))):
-        send_q(part.at[cx, rows], part.at[0, rows], (d_next, tile))
-        send_q(part.at[1, rows], part.at[cx + 1, rows], (d_prev, tile))
-    send_q(q_high.at[cx, 1], q_low.at[0, 0], (d_next, t_next))
-    send_q(q_low.at[cx, 1], q_high.at[0, 2], (d_next, t_prev))
-    send_q(q_high.at[1, 1], q_low.at[cx + 1, 0], (d_prev, t_next))
-    send_q(q_low.at[1, 1], q_high.at[cx + 1, 2], (d_prev, t_prev))
-
-    for copy in q_sends[:inner_sends]:
+
+        @pl.when(tile == 0)
+        def _():
+            u[:, 2 + h * half : 2 + h * half + half, 0:2] = jnp.zeros(
+                (3, half, 2, CHUNKS, LANES), jnp.float32)
+
+        @pl.when(tile == nt - 1)
+        def _():
+            u[:, 2 + h * half : 2 + h * half + half, cy + 2 : cy + 4] = jnp.zeros(
+                (3, half, 2, CHUNKS, LANES), jnp.float32)
+
+        def both(x, carry):
+            q_rows(u, gz, raw, x, 0, 2)
+            q_rows(u, gz, raw, x, cy - 2, 2)
+            return carry
+
+        lax.fori_loop(h * half, h * half + half, both, 0)
+        own_q, own_raw = pl.ds(1 + h * half, half), pl.ds(h * half, half)
+        q_low[own_q, 1:3] = along_z(raw[own_raw, 0:2], smoother)
+        q_high[own_q, 0:2] = along_z(raw[own_raw, cy - 2 : cy], smoother)
+        send_q(q_high.at[own_q, 1], q_low.at[own_q, 0], (depth, t_next), rim_sends)
+        send_q(q_low.at[own_q, 1], q_high.at[own_q, 2], (depth, t_prev), rim_sends)
+        at, to, device = (1, cx + 1, d_prev) if h == 0 else (cx, 0, d_next)
+        send_q(q_low.at[at, pl.ds(1, 2)], q_low.at[to, pl.ds(1, 2)], (device, tile), rim_sends)
+        send_q(q_high.at[at, pl.ds(0, 2)], q_high.at[to, pl.ds(0, 2)], (device, tile), rim_sends)
+        send_q(q_high.at[at, 1], q_low.at[to, 0], (device, t_next), rim_sends)
+        send_q(q_low.at[at, 1], q_high.at[to, 2], (device, t_prev), rim_sends)
+
+    lax.fori_loop(0, inner // 2, inside, 0)
+    for b in (0, 3):
+        x_arrived(b)
+        outside(b)
+    lax.fori_loop(inner // 2, inner, inside, 0)
+    for b in (1, 2, 4):
+        x_arrived(b)
+    outside(4)
+    rim(0)
+    rim(1)
+
+    for copy in q_sends:
         copy.wait_recv()
 
     @pl.when(depth == 0)
@@ -277,6 +287,11 @@
 
     def along(view):
         return view + flip * (cx - 1 - 2 * view)
+
+    def image_row(y):
+        if isinstance(y, int):
+            return y - 4 if 4 <= y < cy - 4 else (y + cy - 8 if y < 4 else y)
+        return y - 4
 
     def composite(y, rows, span_of, unroll):
         def y_blurred(x):
@@ -306,7 +321,7 @@
         state = lax.fori_loop(0, cx, layer, state, unroll=unroll)
         _, _, trans, sum_a, sum_b, sum_c = state
         covered = 1.0 - trans
-        where = pl.ds(y, rows)
+        where = pl.ds(image_row(y), rows)
         image[0, where] = trans
         image[1, where] = 0.5 * (covered + sum_a)
         image[2, where] = 0.5 * (covered + sum_b)
@@ -320,33 +335,76 @@
 
         lax.fori_loop(0, count // 2, pair, 0)
 
-    def piece(d, par, where, group):
+    chip, core = depth // 2, lax.rem(depth, 2)
+    chips = nd // 2
+
+    def near_copies(group, core_at):
         rows = pl.ds(8 * group, 8)
-        return image.at[:, rows, HALF * par + d], pieces.at[where, :, par, rows]
-
-    def send_image(group):
-        for hop in range(1, nd):
-            for d in range(nd):
-                @pl.when(d == lax.rem(depth + hop, nd))
-                def _(d=d):
-                    for par in range(2):
-                        src, dst = piece(d, par, depth, group)
-                        send(src, dst, is_sem.at[group, d, par], ir_sem.at[group, depth, par], (d, tile))
-        for d in range(nd):
-            @pl.when(depth == d)
-            def _(d=d):
-                for par in range(2):
-                    src, dst = piece(d, par, depth, group)
-                    pltpu.make_async_copy(src, dst, own_sem.at[group, par]).start()
-
-    groups = cy // 8
-    for group in range(1, groups - 1):
-        middle_rows(8 * group, 8)
-        send_image(group)
-    middle_rows(4, 4)
-    middle_rows(cy - 8, 4)
-
-    for copy in q_sends[inner_sends:]:
+        give, keep = [], []
+        for to in range(chips):
+            for par in range(2):
+                k = 2 * to + par
+                dst = near.at[core_at, to, :, par, rows]
+                src = image.at[:, rows, HALF * par + 2 * to + (1 - core_at)]
+                give.append(pltpu.make_async_remote_copy(
+                    src_ref=src, dst_ref=dst, send_sem=is_sem.at[group, k],
+                    recv_sem=ir_sem.at[group, k], device_id=(2 * chip + (1 - core_at), tile),
+                    device_id_type=MESH))
+                src = image.at[:, rows, HALF * par + 2 * to + core_at]
+                keep.append(pltpu.make_async_copy(src, dst, own_sem.at[group, k]))
+        return give, keep
+
+    def send_near(group):
+        for core_at in range(2):
+            @pl.when(core == core_at)
+            def _(core_at=core_at):
+                for copies in near_copies(group, core_at):
+                    for copy in copies:
+                        copy.start()
+
+    def far_copy(group, to, source):
+        rows = pl.ds(8 * group, 8)
+        return pltpu.make_async_remote_copy(
+            src_ref=merged.at[to, :, :, rows], dst_ref=far.at[source, :, :, rows],
+            send_sem=fs_sem.at[group, to], recv_sem=fr_sem.at[group, source],
+            device_id=(2 * to + core, tile), device_id_type=MESH)
+
+    def merge_near(group):
+        for core_at in range(2):
+            @pl.when(core == core_at)
+            def _(core_at=core_at):
+                for copies in near_copies(group, core_at):
+                    for copy in copies:
+                        copy.wait()
+        rows = pl.ds(8 * group, 8)
+        straight = flip == 0
+        for to in range(chips):
+            one, two = near[0, to, :, :, rows], near[1, to, :, :, rows]
+            front, back = jnp.where(straight, one, two), jnp.where(straight, two, one)
+            trans = front[0] * back[0]
+            shade = front[1:] + front[0][None] * back[1:]
+            merged[to, 0, :, rows] = trans
+            merged[to, 1:4, :, rows] = shade
+
+            @pl.when(chip == to)
+            def _(to=to, trans=trans, shade=shade):
+                far[to, 0, :, rows] = trans
+                far[to, 1:4, :, rows] = shade
+        for to in range(chips):
+            @pl.when(chip != to)
+            def _(to=to):
+                far_copy(group, to, chip).start()
+
+    middle_rows(4, 8)
+    send_near(0)
+    middle_rows(12, 8)
+    send_near(1)
+    merge_near(0)
+    middle_rows(20, 8)
+    send_near(2)
+    merge_near(1)
+
+    for copy in rim_sends:
         copy.wait_recv()
 
     @pl.when(depth == 0)
@@ -368,49 +426,36 @@
         q_high[:, 2] = jnp.zeros((cx + 2, CHUNKS, LANES), jnp.float32)
 
     composite(0, 4, lambda x: jnp.concatenate([q_low[x + 1], q[x + 1, 0:3]], axis=0), 2)
-    send_image(0)
     composite(cy - 4, 4, lambda x: jnp.concatenate(
         [q[x + 1, mid - 3 : mid], q_high[x + 1]], axis=0), 2)
-    send_image(groups - 1)
-
-    for group in list(range(1, groups - 1)) + [0, groups - 1]:
-        for d in range(nd):
-            @pl.when(depth != d)
-            def _(d=d, group=group):
-                for par in range(2):
-                    src, _ = piece(d, par, depth, group)
-                    _, dst = piece(d, par, d, group)
-                    pltpu.make_async_remote_copy(
-                        src_ref=src, dst_ref=dst, send_sem=is_sem.at[group, d, par],
-                        recv_sem=ir_sem.at[group, d, par], device_id=(d, tile),
-                        device_id_type=MESH).wait()
-
-            @pl.when(depth == d)
-            def _(d=d, group=group):
-                for par in range(2):
-                    src, dst = piece(d, par, d, group)
-                    pltpu.make_async_copy(src, dst, own_sem.at[group, par]).wait()
-
-    total = None
-    for view in range(nd):
-        part = pieces[view + flip * (nd - 1 - 2 * view)]
-        if total is None:
+    send_near(3)
+    merge_near(2)
+    merge_near(3)
+
+    for group in range(4):
+        for to in range(chips):
+            @pl.when(chip != to)
+            def _(group=group, to=to):
+                far_copy(group, to, to).wait()
+
+    trans = shade = None
+    for view in range(chips):
+        part = far[view + flip * (chips - 1 - 2 * view)]
+        if trans is None:
             trans, shade = part[0], part[1:]
         else:
             shade = shade + trans[None] * part[1:]
             trans = trans * part[0]
-        total = view
     for par in range(2):
         lanes = slice(par * LANES, (par + 1) * LANES)
-        color[:, :, lanes] = shade[:, par]
-        alpha[:, lanes] = 1.0 - trans[par]
-
-    for pair in x_sends:
+        for y0, at, ny in ((4, 0, cy - 8), (0, cy - 8, 4), (cy - 4, cy - 4, 4)):
+            result[1:4, y0 : y0 + ny, lanes] = shade[:, par, at : at + ny]
+            result[0, y0 : y0 + ny, lanes] = 1.0 - trans[par, at : at + ny]
+
+    for pair in list(x_sends.values()) + list(y_sends.values()):
         for copy in pair:
             copy.wait_send()
-    for copy in y_sends:
-        copy.wait_send()
-    for copy in q_sends:
+    for copy in q_sends + rim_sends:
         copy.wait_send()
 
 
@@ -425,21 +470,15 @@
         def body(*refs):
             kernel(nd, nt, cx, cy, *refs)
 
-        return pl.pallas_call(
+        result = pl.pallas_call(
             body,
-            out_shape=(
-                jax.ShapeDtypeStruct((3, cy, width), jnp.float32),
-                jax.ShapeDtypeStruct((cy, width), jnp.float32),
-            ),
+            out_shape=jax.ShapeDtypeStruct((4, cy, width), jnp.float32),
             in_specs=[
                 pl.BlockSpec(memory_space=pl.ANY),
                 pl.BlockSpec(memory_space=pltpu.SMEM),
                 pl.BlockSpec(memory_space=pltpu.VMEM),
             ],
-            out_specs=(
-                pl.BlockSpec(memory_space=pltpu.VMEM),
-                pl.BlockSpec(memory_space=pltpu.VMEM),
-            ),
+            out_specs=pl.BlockSpec(memory_space=pltpu.VMEM),
             scratch_shapes=[
                 pltpu.VMEM((3, cx + 4, cy + 4, CHUNKS, LANES), jnp.float32),
                 pltpu.VMEM((3, cx, cy, CHUNKS, LANES), jnp.float32),
@@ -451,15 +490,30 @@
                 pltpu.VMEM((6 * LANES, 2 * LANES), jnp.bfloat16),
                 pltpu.VMEM((cx // 8, cy // 4, CHUNKS, LANES), jnp.float32),
                 pltpu.VMEM((4, cy, CHUNKS, LANES), jnp.float32),
-                pltpu.VMEM((nd, 4, 2, cy, width // 2), jnp.float32),
+                pltpu.VMEM((2, nd // 2, 4, 2, cy, LANES), jnp.float32),
+                pltpu.VMEM((nd // 2, 4, 2, cy, LANES), jnp.float32),
+                pltpu.VMEM((nd // 2, 4, 2, cy, LANES), jnp.float32),
                 dma((5,)),
-                dma((2, 4)), dma((2, 4)), dma((2,)), dma((2,)),
-                dma((14,)), dma((14,)), dma((cy // 8, nd, 2)), dma((cy // 8, nd, 2)), dma((cy // 8, 2)),
+                dma((2, 5)), dma((2, 5)), dma((2, 2)), dma((2, 2)),
+                dma((18,)), dma((18,)), dma((cy // 8, nd)), dma((cy // 8, nd)), dma((cy // 8, nd)),
+                dma((cy // 8, nd // 2)), dma((cy // 8, nd // 2)),
             ],
             compiler_params=pltpu.CompilerParams(
                 collective_id=0, has_side_effects=True, vmem_limit_bytes=56 << 20
             ),
         )(velocity, view_sign, brick_flags)
+
+        def hand_over(result_ref, color_ref, alpha_ref):
+            color_ref[...] = result_ref[1:4]
+            alpha_ref[...] = result_ref[0]
+
+        return pl.pallas_call(
+            hand_over,
+            out_shape=(
+                jax.ShapeDtypeStruct((3, cy, width), jnp.float32),
+                jax.ShapeDtypeStruct((cy, width), jnp.float32),
+            ),
+        )(result)
 
     placed = (P(None, "depth", "tile", None), P("tile"), P("depth", "tile", None))
     return jax.shard_map(

time: 55.5 us -> 51.2 us (0.923)
  local copies, waits for them, and re-layouts: 2.91 us -> 0 us
  Pallas kernels: 51 us -> 49.7 us
    unnamed x2 -> x0, local copies, waits for them, and re-layouts: 2.91 us -> none
    pallas_call x1 -> x2, Pallas kernels: 51 us -> 49.7 us  [the longest x1 48.1 us: per_device(): pl.pallas_call(body, out_shape=jax.ShapeDtypeStruct((4, cy, width), jnp.f...]
where the time goes in v3:
time: 51.2 us; the launch traced here: 51 us
  Pallas kernels  49.7 us (97%)
  between operations  1.28 us (2%)
    pallas_call x1, Pallas kernels, per_device(): pl.pallas_call(body, out_shape=jax.ShapeDtypeStruct((4, cy, width), jnp.f...  48.1 us
    pallas_call x1, Pallas kernels, per_device(): pl.pallas_call(hand_over, out_shape=(jax.ShapeDtypeStruct((3, cy, width),...  1.56 us

profile of v3, /device:TPU:1, one launch (start us, length us, event | category | flops | bytes accessed | tf_op | source)
XLA Modules:
  0.0 51.0 jit_solution(10356490765144675802)
XLA Ops:
  1.3 48.1 %shard_map.50.result_ref = f32[4,32,256]{2,1,0:T(8,128)} custom-call(f32[3,16,32,2048]{3,2,1,0:T(8,128)} %refs_0_.1, s32[1]{0:T(128)S(6)} %copy.5.refs_1_, s32[2,8,16]{2,1,0:T(8,128)} %refs_2_.1), custom_call_target="tpu_custom_call" | custom-call | tf_op jit(solution)/shard_map/pallas_call | solution.py:473
  49.4 1.6 %shard_map.51 = (f32[3,32,256]{2,1,0:T(8,128)}, f32[32,256]{1,0:T(8,128)}) custom-call(f32[4,32,256]{2,1,0:T(8,128)} %shard_map.50.result_ref), custom_call_target="tpu_custom_call" | custom-call | tf_op jit(solution)/shard_map/pallas_call | solution.py:510

commit v4 on v3

--- a/solution.py
+++ b/solution.py
@@ -73,7 +73,7 @@
 
 def kernel(
     nd, nt, cx, cy, vel, sign, bricks, result,
-    u, gz, raw, q, q_low, q_high, slope, smoother, flags, image, near, merged, far, load_sem,
+    u, gz, glow, raw, q, face_a, face_b, q_low, q_high, slope, smoother, flags, image, near, merged, far, load_sem,
     xs_sem, xr_sem, ys_sem, yr_sem, qs_sem, qr_sem, is_sem, ir_sem, own_sem, fs_sem, fr_sem,
 ):
     depth, tile = lax.axis_index("depth"), lax.axis_index("tile")
@@ -99,15 +99,14 @@
     faces = ((0, cx - 2, 2, 0, cy), (1, 0, 2, 0, cy))
     edges = ((2, 2, inner, 0, 8), (3, 2, inner, cy - 8, 8))
     middle = (4, 2, inner, 8, cy - 16)
-    for group in faces + edges + (middle,):
-        load(*group)
-
     around = [(d_next, tile), (d_prev, tile), (depth, t_next), (depth, t_prev),
               (d_next, t_next), (d_next, t_prev), (d_prev, t_next), (d_prev, t_prev)]
     around += [(lax.rem(depth + hop, nd), tile) for hop in range(2, nd, 2)]
     barrier = pltpu.get_barrier_semaphore()
     for device in around:
         pl.semaphore_signal(barrier, inc=1, device_id=device, device_id_type=MESH)
+    for group in faces + edges + (middle,):
+        load(*group)
     pl.semaphore_wait(barrier, len(around))
 
     def send(src, dst, s_sem, r_sem, device):
@@ -118,7 +117,7 @@
         copy.start()
         return copy
 
-    bands = ((10, cy - 20), (0, 2), (cy - 2, 2), (2, 8), (cy - 10, 8))
+    bands = ((2, cy - 12), (0, 2), (cy - 2, 2), (cy - 10, 8))
     for group in faces:
         loaded(*group)
     x_sends, y_sends = {}, {}
@@ -144,8 +143,8 @@
                  ys_sem.at[1, h], yr_sem.at[1, h], (depth, t_prev)),
         )
 
-    issue_x(0)
-    issue_x(3)
+    for b in (0, 1, 2):
+        issue_x(b)
     for group in edges:
         loaded(*group)
     issue_y(0)
@@ -175,10 +174,20 @@
         return carry
 
     lax.fori_loop(0, cx, z_plane, 0)
-    for b in (1, 2, 4):
-        issue_x(b)
+    issue_x(3)
     issue_y(1)
 
+    def glow_plane(x, carry):
+        def speed(k, carry):
+            rows = pl.ds(4 * k, 4)
+            squares = [u[comp, x + 2, pl.ds(4 * k + 2, 4)] for comp in range(3)]
+            squares = [v * v for v in squares]
+            glow[x, rows] = jnp.tanh(0.5 * (squares[0] + squares[1] + squares[2]) - 1.5)
+            return carry
+
+        return lax.fori_loop(0, cy // 4, speed, carry)
+
+    lax.fori_loop(0, cx, glow_plane, 0)
     big = 4
 
     def inside(step, carry):
@@ -189,7 +198,7 @@
             return carry
 
         lax.fori_loop(0, mid // big, block, 0)
-        q[x + 1] = along_z(raw[x, pl.ds(2, mid)], smoother)
+        q[x] = along_z(raw[x, pl.ds(2, mid)], smoother)
         return carry
 
     def face_x(i):
@@ -225,9 +234,10 @@
         lax.fori_loop(0, 4 * (ny // big), block, 0)
         rows = pl.ds(y0 - 2, ny)
         for x0 in (0, cx - 2):
-            q[pl.ds(x0 + 1, 2), rows] = along_z(raw[pl.ds(x0, 2), pl.ds(y0, ny)], smoother)
-        send_q(q.at[cx, rows], q.at[0, rows], (d_next, tile), q_sends)
-        send_q(q.at[1, rows], q.at[cx + 1, rows], (d_prev, tile), q_sends)
+            q[pl.ds(x0, 2), rows] = along_z(raw[pl.ds(x0, 2), pl.ds(y0, ny)], smoother)
+        face = face_a if b == 0 else face_b
+        send_q(q.at[cx - 1, rows], face.at[0], (d_next, tile), q_sends)
+        send_q(q.at[0, rows], face.at[1], (d_prev, tile), q_sends)
 
     def rim(h):
         for copy in y_sends[h]:
@@ -260,28 +270,6 @@
         send_q(q_high.at[at, 1], q_low.at[to, 0], (device, t_next), rim_sends)
         send_q(q_low.at[at, 1], q_high.at[to, 2], (device, t_prev), rim_sends)
 
-    lax.fori_loop(0, inner // 2, inside, 0)
-    for b in (0, 3):
-        x_arrived(b)
-        outside(b)
-    lax.fori_loop(inner // 2, inner, inside, 0)
-    for b in (1, 2, 4):
-        x_arrived(b)
-    outside(4)
-    rim(0)
-    rim(1)
-
-    for copy in q_sends:
-        copy.wait_recv()
-
-    @pl.when(depth == 0)
-    def _():
-        q[0] = jnp.zeros((mid, CHUNKS, LANES), jnp.float32)
-
-    @pl.when(depth == nd - 1)
-    def _():
-        q[cx + 1] = jnp.zeros((mid, CHUNKS, LANES), jnp.float32)
-
     flip = sign[0]
     scale = -1.0 / (288.0 * 64.0)
 
@@ -294,31 +282,29 @@
         return y - 4
 
     def composite(y, rows, span_of, unroll):
-        def y_blurred(x):
-            span = span_of(x)
+        def y_blurred(x, face=False):
+            span = span_of(x, face)
             return (span[0:rows] + span[2 : rows + 2]) + 2.0 * span[1 : rows + 1]
 
-        def layer(view, state):
+        def shade_layer(x, after, state):
             before, here, trans, sum_a, sum_b, sum_c = state
-            x = along(view)
-            after = y_blurred(along(view + 1))
             smooth = (before + after) + 2.0 * here
-            v0 = u[0, x + 2, pl.ds(y + 2, rows)]
-            v1 = u[1, x + 2, pl.ds(y + 2, rows)]
-            v2 = u[2, x + 2, pl.ds(y + 2, rows)]
-            speed = v0 * v0 + v1 * v1 + v2 * v2
             peak = flags[x // 8, y // 4][None]
             tanh_q = jnp.tanh(scale * smooth)
             tanh_half = jnp.tanh((0.5 * scale) * smooth)
-            tanh_speed = jnp.tanh(0.5 * speed - 1.5)
+            tanh_speed = glow[x, pl.ds(y, rows)]
             weight = trans * (peak + peak * tanh_q)
             return (here, after, trans - weight, sum_a + weight * tanh_half,
                     sum_b + weight * tanh_speed, sum_c + weight * tanh_q)
 
+        def layer(view, state):
+            return shade_layer(along(view), y_blurred(along(view + 1)), state)
+
         one = jnp.ones((rows, CHUNKS, LANES), jnp.float32)
         zero = jnp.zeros((rows, CHUNKS, LANES), jnp.float32)
-        state = (y_blurred(along(-1)), y_blurred(along(0)), one, zero, zero, zero)
-        state = lax.fori_loop(0, cx, layer, state, unroll=unroll)
+        state = (y_blurred(flip, True), y_blurred(along(0)), one, zero, zero, zero)
+        state = lax.fori_loop(0, cx - 1, layer, state, unroll=unroll)
+        state = shade_layer(along(cx - 1), y_blurred(1 - flip, True), state)
         _, _, trans, sum_a, sum_b, sum_c = state
         covered = 1.0 - trans
         where = pl.ds(image_row(y), rows)
@@ -327,10 +313,36 @@
         image[2, where] = 0.5 * (covered + sum_b)
         image[3, where] = 0.5 * (covered - sum_c)
 
-    def middle_rows(y0, count):
+    def span_a(y):
+        return lambda x, face: (face_a if face else q)[x, pl.ds(y - 3, 4)]
+
+    def span_b(y):
+        return lambda x, face: face_b[x, pl.ds(y - cy + 9, 4)] if face else q[x, pl.ds(y - 3, 4)]
+
+    def span_ab(y):
+        cut = cy - 10 - (y - 1)
+
+        def span(x, face):
+            if not face:
+                return q[x, y - 3 : y + 1]
+            return jnp.concatenate([face_a[x, y - 3 : y - 3 + cut], face_b[x, 0 : 4 - cut]], axis=0)
+
+        return span
+
+    def span_low(x, face):
+        if face:
+            return jnp.concatenate([q_low[x * (cx + 1)], face_a[x, 0:3]], axis=0)
+        return jnp.concatenate([q_low[x + 1], q[x, 0:3]], axis=0)
+
+    def span_high(x, face):
+        if face:
+            return jnp.concatenate([face_b[x, 5:8], q_high[x * (cx + 1)]], axis=0)
+        return jnp.concatenate([q[x, mid - 3 : mid], q_high[x + 1]], axis=0)
+
+    def row_pairs(y0, count, span):
         def pair(k, carry):
             y = y0 + 2 * k
-            composite(y, 2, lambda x: q[x + 1, pl.ds(y - 3, 4)], 4)
+            composite(y, 2, span(y), 5)
             return carry
 
         lax.fori_loop(0, count // 2, pair, 0)
@@ -395,12 +407,38 @@
             def _(to=to):
                 far_copy(group, to, chip).start()
 
-    middle_rows(4, 8)
+    def faces_arrived(copies, face):
+        for copy in copies:
+            copy.wait_recv()
+
+        @pl.when(depth == 0)
+        def _():
+            face[0] = jnp.zeros(face.shape[1:], jnp.float32)
+
+        @pl.when(depth == nd - 1)
+        def _():
+            face[1] = jnp.zeros(face.shape[1:], jnp.float32)
+
+    lax.fori_loop(0, inner // 2, inside, 0)
+    x_arrived(0)
+    outside(0)
+    x_arrived(1)
+    x_arrived(2)
+    rim(0)
+    lax.fori_loop(inner // 2, inner, inside, 0)
+    rim(1)
+    x_arrived(3)
+    outside(3)
+    faces_arrived(q_sends[:2], face_a)
+    row_pairs(4, 8, span_a)
     send_near(0)
-    middle_rows(12, 8)
+    row_pairs(12, 8, span_a)
     send_near(1)
     merge_near(0)
-    middle_rows(20, 8)
+    faces_arrived(q_sends[2:], face_b)
+    composite(cy - 12, 2, span_ab(cy - 12), 5)
+    composite(cy - 10, 2, span_ab(cy - 10), 5)
+    row_pairs(cy - 8, 4, span_b)
     send_near(2)
     merge_near(1)
 
@@ -425,9 +463,8 @@
     def _():
         q_high[:, 2] = jnp.zeros((cx + 2, CHUNKS, LANES), jnp.float32)
 
-    composite(0, 4, lambda x: jnp.concatenate([q_low[x + 1], q[x + 1, 0:3]], axis=0), 2)
-    composite(cy - 4, 4, lambda x: jnp.concatenate(
-        [q[x + 1, mid - 3 : mid], q_high[x + 1]], axis=0), 2)
+    composite(0, 4, span_low, 3)
+    composite(cy - 4, 4, span_high, 3)
     send_near(3)
     merge_near(2)
     merge_near(3)
@@ -483,7 +520,10 @@
                 pltpu.VMEM((3, cx + 4, cy + 4, CHUNKS, LANES), jnp.float32),
                 pltpu.VMEM((3, cx, cy, CHUNKS, LANES), jnp.float32),
                 pltpu.VMEM((cx, cy, CHUNKS, LANES), jnp.float32),
-                pltpu.VMEM((cx + 2, cy - 4, CHUNKS, LANES), jnp.float32),
+                pltpu.VMEM((cx, cy, CHUNKS, LANES), jnp.float32),
+                pltpu.VMEM((cx, cy - 4, CHUNKS, LANES), jnp.float32),
+                pltpu.VMEM((2, cy - 12, CHUNKS, LANES), jnp.float32),
+                pltpu.VMEM((2, 8, CHUNKS, LANES), jnp.float32),
                 pltpu.VMEM((cx + 2, 3, CHUNKS, LANES), jnp.float32),
                 pltpu.VMEM((cx + 2, 3, CHUNKS, LANES), jnp.float32),
                 pltpu.VMEM((6 * LANES, 2 * LANES), jnp.bfloat16),

time: 51.2 us -> 49.6 us (0.969)
  Pallas kernels: 49.7 us -> 48.1 us
    pallas_call x1, Pallas kernels: 48.1 us -> 46.5 us  [per_device(): pl.pallas_call(body, out_shape=jax.ShapeDtypeStruct((4, cy, width), jnp.f...]
where the time goes in v4:
time: 49.6 us; the launch traced here: 49.4 us
  Pallas kernels  48.1 us (97%)
  between operations  1.28 us (3%)
    pallas_call x1, Pallas kernels, per_device(): pl.pallas_call(body, out_shape=jax.ShapeDtypeStruct((4, cy, width), jnp.f...  46.5 us
    pallas_call x1, Pallas kernels, per_device(): pl.pallas_call(hand_over, out_shape=(jax.ShapeDtypeStruct((3, cy, width),...  1.56 us

profile of v4, /device:TPU:1, one launch (start us, length us, event | category | flops | bytes accessed | tf_op | source)
XLA Modules:
  0.0 49.4 jit_solution(12834664765326418503)
XLA Ops:
  1.3 46.5 %shard_map.50.result_ref = f32[4,32,256]{2,1,0:T(8,128)} custom-call(f32[3,16,32,2048]{3,2,1,0:T(8,128)} %refs_0_.1, s32[1]{0:T(128)S(6)} %copy.5.refs_1_, s32[2,8,16]{2,1,0:T(8,128)} %refs_2_.1), custom_call_target="tpu_custom_call" | custom-call | tf_op jit(solution)/shard_map/pallas_call | solution.py:510
  47.8 1.6 %shard_map.51 = (f32[3,32,256]{2,1,0:T(8,128)}, f32[32,256]{1,0:T(8,128)}) custom-call(f32[4,32,256]{2,1,0:T(8,128)} %shard_map.50.result_ref), custom_call_target="tpu_custom_call" | custom-call | tf_op jit(solution)/shard_map/pallas_call | solution.py:550

commit v5 on v4

--- a/solution.py
+++ b/solution.py
@@ -349,6 +349,7 @@
 
     chip, core = depth // 2, lax.rem(depth, 2)
     chips = nd // 2
+    hops = sorted(range(1, chips), key=lambda hop: abs(2 * hop - chips))
 
     def near_copies(group, core_at):
         rows = pl.ds(8 * group, 8)
@@ -402,10 +403,8 @@
             def _(to=to, trans=trans, shade=shade):
                 far[to, 0, :, rows] = trans
                 far[to, 1:4, :, rows] = shade
-        for to in range(chips):
-            @pl.when(chip != to)
-            def _(to=to):
-                far_copy(group, to, chip).start()
+        for hop in hops:
+            far_copy(group, lax.rem(chip + hop, chips), chip).start()
 
     def faces_arrived(copies, face):
         for copy in copies:
@@ -470,10 +469,9 @@
     merge_near(3)
 
     for group in range(4):
-        for to in range(chips):
-            @pl.when(chip != to)
-            def _(group=group, to=to):
-                far_copy(group, to, to).wait()
+        for hop in hops:
+            to = lax.rem(chip + hop, chips)
+            far_copy(group, to, to).wait()
 
     trans = shade = None
     for view in range(chips):

time: 49.6 us -> 49.6 us (level)
  no operation moved by 1% of the time
where the time goes in v5:
time: 49.6 us; the launch traced here: 49.4 us
  Pallas kernels  48.1 us (97%)
  between operations  1.28 us (3%)
    pallas_call x1, Pallas kernels, per_device(): pl.pallas_call(body, out_shape=jax.ShapeDtypeStruct((4, cy, width), jnp.f...  46.5 us
    pallas_call x1, Pallas kernels, per_device(): pl.pallas_call(hand_over, out_shape=(jax.ShapeDtypeStruct((3, cy, width),...  1.56 us

profile of v5, /device:TPU:1, one launch (start us, length us, event | category | flops | bytes accessed | tf_op | source)
XLA Modules:
  0.0 49.4 jit_solution(18411026133897448221)
XLA Ops:
  1.3 46.5 %shard_map.50.result_ref = f32[4,32,256]{2,1,0:T(8,128)} custom-call(f32[3,16,32,2048]{3,2,1,0:T(8,128)} %refs_0_.1, s32[1]{0:T(128)S(6)} %copy.5.refs_1_, s32[2,8,16]{2,1,0:T(8,128)} %refs_2_.1), custom_call_target="tpu_custom_call" | custom-call | tf_op jit(solution)/shard_map/pallas_call | solution.py:508
  47.8 1.6 %shard_map.51 = (f32[3,32,256]{2,1,0:T(8,128)}, f32[32,256]{1,0:T(8,128)}) custom-call(f32[4,32,256]{2,1,0:T(8,128)} %shard_map.50.result_ref), custom_call_target="tpu_custom_call" | custom-call | tf_op jit(solution)/shard_map/pallas_call | solution.py:548
